TPU v7x, 32 devices: a whole 2x2x4 slice. The times are simulated.
32 devices in a mesh: section: 4 (over x, core), fsdp: 8 (over z, y).
Axes of the slice: x: 2, y: 2, z: 4, core: 2. Of those that a mesh axis runs over, the one named last changes fastest.
Arguments:
- section_input: bfloat16 [4, 256, 12288], P('section', None, 'fsdp'), may hold values from -6 to 6
- stash_held: bfloat16 [4, 256, 12288], P('section', None, 'fsdp'), may hold values from -17 to 17
- upstream: bfloat16 [4, 256, 12288], P('section', None, 'fsdp'), may hold values from -6 to 6
- norm_gain: float32 [4, 12288], P('section', 'fsdp'), may hold values from 0.25 to 1.75
- out_weight: bfloat16 [4, 6144, 12288], P('section', None, 'fsdp'), may hold values from -0.078125 to 0.078125
Outputs:
- section_output: bfloat16 [4, 256, 12288], P('section', None, 'fsdp')
- stash_moved: bfloat16 [4, 256, 12288], P('section', None, 'fsdp')
- input_grad: bfloat16 [4, 256, 12288], P('section', None, 'fsdp')
All inputs are finite; a program needn't handle non-finite values.
Results may differ from a plain program's by a relative error of at most 0.012.
The roundings to bfloat16 on the way count: a program that leaves them out, or rounds other values in their place, can miss the bound.
Values may be sent and summed in bfloat16 or wider, within the bound.
No kernel may reach another device: no remote copies, remote signals or barrier semaphores. Data moves between devices by JAX's collectives and lax.ppermute only.
A program may use at most 64 MiB of HBM per device.

v0:
```python
import jax
import jax.numpy as jnp
from jax import lax
from jax.sharding import PartitionSpec as P

D = 12288
HD = 128


EPSILON = 1e-05


def partner(value, axis, distance):
    mask = 2**distance
    pairs = [(source, source ^ mask) for source in range(lax.axis_size(axis))]
    return lax.ppermute(value, axis, pairs)


def attend(normed):
    tokens = normed.shape[0]
    paired = normed.reshape(tokens, normed.shape[1] // (2 * HD), 2, HD)
    queries = paired[:, :, 0]
    keyvals = paired[:, :, 1]
    shrink = HD ** (-0.5)
    scores = (
        jnp.einsum("qhd,khd->hqk", queries, keyvals, preferred_element_type=jnp.float32) * shrink
    )
    row_ids = lax.broadcasted_iota(jnp.int32, (tokens, tokens), 0)
    col_ids = lax.broadcasted_iota(jnp.int32, (tokens, tokens), 1)
    scores = jnp.where((row_ids >= col_ids)[None], scores, -1e30)
    probs = jax.nn.softmax(scores, axis=-1)
    weights = probs.astype(jnp.bfloat16)
    context = jnp.einsum("hqk,khd->qhd", weights, keyvals, preferred_element_type=jnp.float32)
    context = context.astype(jnp.bfloat16).reshape(tokens, -1)
    return (queries, keyvals, probs, weights, context)


def local(section_input, stash_held, upstream, norm_gain, out_weight):
    fresh = section_input[0]
    held = stash_held[0]
    grad_rows = upstream[0]
    gain_row = norm_gain[0]
    weight = out_weight[0]
    stacked = jnp.stack([fresh, held])
    sections = lax.axis_size("section")
    levels = sections.bit_length() - 1
    moved = stacked
    for level in range(levels):
        moved = partner(moved, "section", level)
    parked_out = moved[0]
    fetched = moved[1]
    fresh_f = fresh.astype(jnp.float32)
    held_f = fetched.astype(jnp.float32)
    totals_f, totals_b = lax.psum(
        (jnp.sum(fresh_f * fresh_f, axis=-1), jnp.sum(held_f * held_f, axis=-1)), "fsdp"
    )
    inverse_f = lax.rsqrt(totals_f / D + EPSILON)
    inverse_b = lax.rsqrt(totals_b / D + EPSILON)
    normed_f = (fresh_f * inverse_f[:, None] * gain_row[None]).astype(jnp.bfloat16)
    normed_b = (held_f * inverse_b[:, None] * gain_row[None]).astype(jnp.bfloat16)
    context_own = attend(normed_f)[4]
    weight_rows = weight
    projected = jnp.dot(
        lax.all_gather(context_own, "fsdp", axis=1, tiled=True),
        weight_rows,
        preferred_element_type=jnp.float32,
    )
    output = (fresh_f + projected).astype(jnp.bfloat16)
    queries, keyvals, probs, weights, unused = attend(normed_b)
    head_rows = context_own.shape[1]
    weight_rows = weight
    dcontext_t = lax.psum_scatter(
        lax.dot_general(
            weight_rows, grad_rows, (((1,), (1,)), ((), ())), preferred_element_type=jnp.float32
        ),
        "fsdp",
        scatter_dimension=0,
        tiled=True,
    )
    tokens = fresh.shape[0]
    dcontext = dcontext_t.T.astype(jnp.bfloat16).reshape(tokens, head_rows // HD, HD)
    dprob = jnp.einsum("qhd,khd->hqk", dcontext, keyvals, preferred_element_type=jnp.float32)
    dvalue = jnp.einsum("hqk,qhd->khd", weights, dcontext, preferred_element_type=jnp.float32)
    shrink = HD ** (-0.5)
    dscore = (probs * (dprob - jnp.sum(dprob * probs, axis=-1, keepdims=True)) * shrink).astype(
        jnp.bfloat16
    )
    dquery = jnp.einsum("hqk,khd->qhd", dscore, keyvals, preferred_element_type=jnp.float32)
    dkey = jnp.einsum("hqk,qhd->khd", dscore, queries, preferred_element_type=jnp.float32)
    dnormed = jnp.stack([dquery, dvalue + dkey], axis=2).reshape(tokens, -1)
    scaled = dnormed * gain_row[None]
    moment = lax.psum(jnp.sum(scaled * held_f, axis=-1), "fsdp")
    grad_in = grad_rows.astype(jnp.float32) + inverse_b[:, None] * scaled
    grad_in = grad_in - held_f * (inverse_b**3 * moment / D)[:, None]
    return (output[None], parked_out[None], grad_in.astype(jnp.bfloat16)[None])


def solution(mesh):
    placed = (
        P("section", None, "fsdp"),
        P("section", None, "fsdp"),
        P("section", None, "fsdp"),
        P("section", "fsdp"),
        P("section", None, "fsdp"),
    )
    return jax.shard_map(
        local,
        mesh=mesh,
        in_specs=placed,
        out_specs=(
            P("section", None, "fsdp"),
            P("section", None, "fsdp"),
            P("section", None, "fsdp"),
        ),
        check_vma=False,
    )
```

profile of v0, /device:TPU:0, one launch (start us, length us, event | category | flops | bytes accessed | tf_op | source)
XLA Modules:
  0.0 252.0 jit_solution(17060094830148846679)
XLA Ops:
  7.2 10.9 %fusion.3 = f32[6144,256]{1,0:T(8,128)} fusion(bf16[1,6144,1536]{2,1,0:T(8,128)(2,1)} %param.9, bf16[1,256,1536]{2,1,0:T(8,128)(2,1)} %param.7), kind=kOutput, calls=%fused_computation.3 | convolution fusion | flops 4831838208 | bytes 25952256 | tf_op jit(solution)/shard_map/dot_general | solution.py:73
  18.2 1.0 copy-done.3
  20.0 0.6 collective-permute-start
  20.6 3.2 %collective-permute-done = bf16[2,256,1536]{1,2,0:T(8,128)(2,1)} collective-permute-done((bf16[2,256,1536]{1,2,0:T(8,128)(2,1)S(1)}, bf16[2,256,1536]{1,2,0:T(8,128)(2,1)}, u32[]{:S(2)}, u32[]{:S(2)}) %collective-permute-start) | collective-permute-done | bytes 1572896 | tf_op jit(solution)/shard_map/ppermute | solution.py:16
  23.7 2.9 %collective-permute-start.1 = (bf16[2,256,1536]{1,2,0:T(8,128)(2,1)}, bf16[2,256,1536]{1,2,0:T(8,128)(2,1)S(1)}, u32[]{:S(2)}, u32[]{:S(2)}) collective-permute-start(bf16[2,256,1536]{1,2,0:T(8,128)(2,1)} %collective-permute-done), channel_id=1, source_target_pairs={{0,16},{8,24},{16,0},{24,8},{1,17},{9,25},{17,1},{25,9},{2,18},{10... | collective-permute-start | bytes 4718600 | tf_op jit(solution)/shard_map/ppermute | solution.py:16
  26.6 1.4 copy.17
  28.0 3.1 %copy.18 = f32[256,6,2,128]{3,0,1,2:T(8,128)} copy(f32[256,6,2,128]{0,3,2,1:T(8,128)} %bitcast.92) | data formatting | bytes 3145728 | tf_op jit(solution)/shard_map/convert_element_type | solution.py:52
  31.4 30.0 %collective-permute-done.1 = bf16[2,256,1536]{1,2,0:T(8,128)(2,1)S(1)} collective-permute-done((bf16[2,256,1536]{1,2,0:T(8,128)(2,1)}, bf16[2,256,1536]{1,2,0:T(8,128)(2,1)S(1)}, u32[]{:S(2)}, u32[]{:S(2)}) %collective-permute-start.1) | collective-permute-done | bytes 1572896 | tf_op jit(solution)/shard_map/ppermute | solution.py:16
  61.5 1.7 fusion.62
  63.2 3.0 %copy.25 = f32[256,6,2,128]{3,0,1,2:T(8,128)} copy(f32[256,6,2,128]{0,3,2,1:T(8,128)} %bitcast.93) | data formatting | bytes 3145728 | tf_op jit(solution)/shard_map/convert_element_type | solution.py:53
  66.4 22.4 %psum.22 = f32[256]{0:T(256)S(1)} all-reduce(f32[256]{0:T(256)S(1)} %multiply_reduce_fusion.2), channel_id=1, replica_groups=mesh['section'=4,'fsdp'=8] {'fsdp'}, use_global_device_ids=true, to_apply=%region_5.6 | all-reduce | flops 256 | bytes 2048 | tf_op jit(solution)/shard_map/psum | solution.py:54
  88.9 1.7 multiply_convert_fusion.1
  90.6 1.8 fusion.63
  92.4 47.5 %reduce-scatter.2.cloned.1.call-done = f32[768,256]{1,0:T(8,128)} async-done(((f32[6144,256]{1,0:T(8,128)}), f32[768,256]{1,0:T(8,128)}) %reduce-scatter.2.cloned.1.call-update) | async-done | bytes 786448 | tf_op jit(solution)/shard_map/reduce_scatter | solution.py:72
  139.9 1.3 convert_element_type.79
  141.2 0.3 fusion.44
  141.6 1.3 fusion.40
  142.9 3.4 %fusion.30 = f32[256,6,1,128]{0,3,1,2:T(8,128)} fusion(f32[6,256,256]{1,2,0:T(8,128)S(1)} %fusion.44, bf16[256,6,2,128]{3,0,1,2:T(8,128)(2,1)S(1)} %multiply_convert_fusion.1, f32[6,256,256]{1,2,0:T(8,128)} %get-tuple-element.11, f32[6,256]{1,0:T(8,128)S(1)} %get-tuple-element.10), kind=kOutput, calls=%fused_computation.31 | convolution fusion | flops 103417600 | bytes 7487488 | tf_op jit(solution)/shard_map/hqk,khd->qhd/dot_general | solution.py:88
  146.3 3.6 %fusion.36 = f32[256,6,1,128]{0,3,1,2:T(8,128)} fusion(f32[6,128,256]{2,1,0:T(8,128)} %fusion.40, f32[6,256,256]{1,2,0:T(8,128)S(1)} %fusion.44, bf16[256,6,2,128]{3,0,1,2:T(8,128)(2,1)S(1)} %multiply_convert_fusion.1, f32[6,256,256]{1,2,0:T(8,128)} %get-tuple-element.11, f32[6,256]{1,0:T(8,128)S(1)} %get-tuple-element.10), kind=kOutput, calls=%fused_computation.33 | convolution fusion | flops 103614208 | bytes 8273920 | tf_op jit(solution)/shard_map/hqk,qhd->khd/dot_general | solution.py:89
  149.9 1.5 pad_maximum_fusion.1
  151.6 1.3 copy-done.2
  152.9 0.3 multiply_reduce_fusion
  153.2 19.9 %all-reduce = (f32[256]{0:T(256)S(1)}, f32[256]{0:T(256)S(1)}) all-reduce(f32[256]{0:T(256)S(1)} %fusion.18, f32[256]{0:T(256)S(1)} %multiply_reduce_fusion), channel_id=1, replica_groups=mesh['section'=4,'fsdp'=8] {'fsdp'}, use_global_device_ids=true, to_apply=%region_1.0 | all-reduce | flops 512 | bytes 4096 | tf_op jit(solution)/shard_map/psum | solution.py:54
  173.1 1.7 multiply_convert_fusion.2
  174.8 0.6 fusion.64
  175.4 1.7 convolution_convert_fusion
  177.1 1.4 copy.24
  178.5 2.3 copy.33
  180.8 2.5 subtract_convert_fusion
  183.3 2.3 copy.34
  185.6 48.9 %all-gather.2.cloned.1.call-done = bf16[256,6144]{0,1:T(8,128)(2,1)} async-done(((bf16[256,768]{0,1:T(8,128)(2,1)}), bf16[256,6144]{0,1:T(8,128)(2,1)}) %all-gather.2.cloned.1.call-update) | async-done | bytes 3145744 | tf_op jit(solution)/shard_map/all_gather | solution.py:64
  234.5 10.6 %fusion.13 = bf16[1,256,1536]{2,1,0:T(8,128)(2,1)} fusion(bf16[256,6144]{0,1:T(8,128)(2,1)} %all-gather.2.cloned.1.call-done, bf16[1,6144,1536]{2,1,0:T(8,128)(2,1)} %param.9, bf16[1,256,1536]{2,1,0:T(8,128)(2,1)S(1)} %copy-done), kind=kOutput, calls=%fused_computation.9 | convolution fusion | flops 4833017856 | bytes 23592960 | tf_op jit(solution)/shard_map/dot_general | solution.py:63
  (25 shorter events, 1.5 us)
Async XLA Ops:
  7.2 132.7 %reduce-scatter.2.cloned.1.call-start = ((), (), s32[]{:S(2)}) async-start(), calls=%async_computation.2 | async-start | bytes 7077888 | tf_op jit(solution)/shard_map/reduce_scatter | solution.py:72
  18.2 1.1 copy-start.3
  18.2 1.4 copy-start
  18.2 216.3 %all-gather.2.cloned.1.call-start = ((), (), s32[]{:S(2)}) async-start(), calls=%async_computation.1 | async-start | bytes 3538944 | tf_op jit(solution)/shard_map/all_gather | solution.py:64
  20.0 3.7 %collective-permute-start = (bf16[2,256,1536]{1,2,0:T(8,128)(2,1)S(1)}, bf16[2,256,1536]{1,2,0:T(8,128)(2,1)}, u32[]{:S(2)}, u32[]{:S(2)}) collective-permute-start(bf16[2,256,1536]{1,2,0:T(8,128)(2,1)S(1)} %pad_maximum_fusion), channel_id=1, source_target_pairs={{0,8},{8,0},{16,24},{24,16},{1,9},{9,1},{17,25},{25,17},{2,10},{10... | collective-permute-start | bytes 4718600 | tf_op jit(solution)/shard_map/ppermute | solution.py:16
  23.7 37.8 %collective-permute-start.1 = (bf16[2,256,1536]{1,2,0:T(8,128)(2,1)}, bf16[2,256,1536]{1,2,0:T(8,128)(2,1)S(1)}, u32[]{:S(2)}, u32[]{:S(2)}) collective-permute-start(bf16[2,256,1536]{1,2,0:T(8,128)(2,1)} %collective-permute-done), channel_id=1, source_target_pairs={{0,16},{8,24},{16,0},{24,8},{1,17},{9,25},{17,1},{25,9},{2,18},{10... | collective-permute-start | bytes 4718600 | tf_op jit(solution)/shard_map/ppermute | solution.py:16
  28.0 3.1 %copy-start.4 = (f32[1,1536]{1,0:T(1,128)S(1)}, f32[1,1536]{1,0:T(1,128)}, u32[]{:S(2)}) copy-start(f32[1,1536]{1,0:T(1,128)} %param.8) | copy-start | bytes 18436
  61.5 4.7 %copy-start.1 = (bf16[2,256,1536]{1,2,0:T(8,128)(2,1)}, bf16[2,256,1536]{1,2,0:T(8,128)(2,1)S(1)}, u32[]{:S(2)}) copy-start(bf16[2,256,1536]{1,2,0:T(8,128)(2,1)S(1)} %collective-permute-done.1) | copy-start | bytes 4718596
  139.9 1.7 copy-start.5
  151.4 1.4 copy-start.2
Sparse Core Ops, SparseCore 0:
  18.3 121.5 reduce-scatter.1
  177.2 57.2 all-gather.1
where the time goes:
time: 253 us; the launch traced here: 252 us
  waiting for transfers between devices  130 us (51%)
  blocking collectives  42.3 us (17%)
  matrix products  34.4 us (14%)
  local copies, waits for them, and re-layouts  16.5 us (7%)
  between operations  14.2 us (6%)
  other arithmetic  11.4 us (5%)
  starting transfers between devices  3.5 us (1%)
    all_gather x1, waiting for transfers between devices, local(): lax.all_gather(context_own, 'fsdp', axis=1, tiled=True)  48.9 us
    reduce_scatter x1, waiting for transfers between devices, local(): lax.psum_scatter(lax.dot_general(weight_rows, grad_rows, (((1,), (1,)), (...  47.5 us
    psum x2, blocking collectives, local(): lax.psum((jnp.sum(fresh_f * fresh_f, axis=-1), jnp.sum(held_f * held_f, a...  42.3 us
    ppermute x2, waiting for transfers between devices, partner(): return lax.ppermute(value, axis, pairs)  33.2 us
    dot_general x1, matrix products, local(): lax.dot_general(weight_rows, grad_rows, (((1,), (1,)), ((), ())), preferr...  10.9 us
    dot_general x1, matrix products, local(): jnp.dot(lax.all_gather(context_own, 'fsdp', axis=1, tiled=True), weight_r...  10.6 us
    unnamed x17, local copies, waits for them, and re-layouts  8.88 us
  transfers between devices with their start and end apart: 4, of which 4 were waited for; matrix products, arithmetic and copies ran while one was open for 9% of the time, Pallas kernels for 0%

commit v1 on v0

v1 whole, which is shorter than its diff:
```python
import functools

import jax
import jax.numpy as jnp
import numpy as np
from jax import lax
from jax.experimental import pallas as pl
from jax.experimental.pallas import tpu as pltpu
from jax.sharding import PartitionSpec as P

HD = 128
EPSILON = 1e-05
SHRINK = HD ** (-0.5)
F32 = jnp.float32
BF16 = jnp.bfloat16


def ring_order(mesh):
    count = mesh.shape["fsdp"]
    at = list(mesh.axis_names).index("fsdp")
    line = np.moveaxis(mesh.devices, at, 0).reshape(count, -1)[:, 0]
    coords = [getattr(d, "coords", None) for d in line]
    if any(c is None for c in coords):
        return list(range(count))
    inner = sum(1 for c in coords if c[2] == coords[0][2])
    if count % inner or (inner > 1 and inner % 2):
        return list(range(count))
    outer = count // inner
    if inner == 1 or outer == 1:
        return list(range(count))
    order = [z * inner for z in range(outer)]
    for y in range(inner - 1, 0, -1):
        rows = range(outer - 1, 0, -1) if (inner - 1 - y) % 2 == 0 else range(1, outer)
        order += [z * inner + y for z in rows]
    if inner == 2:
        return order + [1]
    return order + [y for y in range(inner - 1, 0, -1)]


VMEM = pl.BlockSpec(memory_space=pltpu.VMEM)
ANY = pl.BlockSpec(memory_space=pl.ANY)
ROOM = 12 * 2**20


def run(kernel, operands, results, after=(), room=ROOM):
    def body(*refs):
        kernel(*refs[: len(operands)], *refs[len(operands) + len(after) :])

    return pl.pallas_call(
        body,
        in_specs=[VMEM] * (len(operands) + len(after)),
        out_specs=[VMEM] * len(results),
        out_shape=[pltpu.VMEM(shape, kind) for shape, kind in results],
        compiler_params=pltpu.CompilerParams(vmem_limit_bytes=room),
    )(*operands, *after)


def causal(tokens):
    rows = lax.broadcasted_iota(jnp.int32, (tokens, tokens), 0)
    cols = lax.broadcasted_iota(jnp.int32, (tokens, tokens), 1)
    return rows >= cols


def as_column(row):
    return jnp.broadcast_to(row, (HD, row.shape[1])).T


def as_row(columns):
    return jnp.sum(columns.T, axis=0, keepdims=True)


def dot(a, b, dims):
    return lax.dot_general(a, b, (dims, ((), ())), preferred_element_type=F32)


def first_row(plan, offset, chunk):
    me = lax.axis_index("fsdp")
    row = jnp.int32(0)
    for device, owner in enumerate(plan[offset]):
        row = jnp.where(me == device, owner * chunk, row)
    return pl.multiple_of(row, chunk)


def begin(plan, fresh, held, rows, weight, chunk, opposite):
    tokens, depth = rows.shape
    count = len(plan[0])

    def body(fresh_ref, held_ref, rows_ref, weight_ref, *rest):
        outs, (fresh_v, held_v, rows_v, weight_v, sems) = rest[:-5], rest[-5:]
        copies = [
            pltpu.make_async_copy(fresh_ref, fresh_v, sems.at[2]),
            pltpu.make_async_copy(held_ref, held_v, sems.at[3]),
        ]
        if opposite:
            at = first_row(plan, count // 2, chunk)
            near = [
                pltpu.make_async_copy(rows_ref, rows_v, sems.at[0]),
                pltpu.make_async_copy(weight_ref.at[pl.ds(at, chunk), :], weight_v, sems.at[1]),
            ]
            for copy in near:
                copy.start()
        for copy in copies:
            copy.start()
        for slot, (copy, ref) in enumerate(zip(copies, (fresh_v, held_v))):
            copy.wait()
            total = jnp.zeros((tokens, HD), F32)
            for start in range(0, depth, HD):
                part = ref[:, start : start + HD].astype(F32)
                total = total + part * part
            outs[0][slot : slot + 1, :] = as_row(total)
        if opposite:
            for copy in near:
                copy.wait()
            for out, start in zip(outs[1:], (0, tokens // 2)):
                part = rows_v[start : start + tokens // 2, :]
                out[...] = dot(part, weight_v[...], ((1,), (1,))).astype(BF16)

    results = [((2, tokens), F32)]
    if opposite:
        results += [((tokens // 2, chunk), BF16)] * 2
    return pl.pallas_call(
        body,
        in_specs=[ANY] * 4,
        out_specs=[VMEM] * len(results),
        out_shape=[pltpu.VMEM(shape, kind) for shape, kind in results],
        scratch_shapes=[
            pltpu.VMEM((tokens, depth), BF16),
            pltpu.VMEM((tokens, depth), BF16),
            pltpu.VMEM((tokens, depth), BF16),
            pltpu.VMEM((chunk, depth), BF16),
            pltpu.SemaphoreType.DMA((4,)),
        ],
        compiler_params=pltpu.CompilerParams(vmem_limit_bytes=ROOM),
        name="begin",
    )(fresh, held, rows, weight)


def partial_sums(plan, rows, weight, offsets, chunk, after):
    def kernel(rows_ref, weight_ref, *outs):
        for offset, out in zip(offsets, outs):
            at = first_row(plan, offset, chunk)
            out[...] = dot(rows_ref[...], weight_ref[pl.ds(at, chunk), :], ((1,), (1,)))

    results = [((rows.shape[0], chunk), F32)] * len(offsets)
    return run(kernel, (rows, weight), results, after)


def add_arrived(ahead, behind, up, down, after):
    def kernel(ahead_ref, behind_ref, *refs):
        half = ahead_ref.shape[0] // 2
        if up is None:
            refs[0][...] = ahead_ref[...].astype(BF16)
            refs[1][...] = behind_ref[...].astype(BF16)
            return
        up_ref, down_ref, to_up, to_down = refs
        if up_ref.shape[0] == half:
            to_up[:half] = (ahead_ref[:half] + up_ref[...].astype(F32)).astype(BF16)
            to_up[half:] = ahead_ref[half:].astype(BF16)
            to_down[:half] = behind_ref[:half].astype(BF16)
            to_down[half:] = (behind_ref[half:] + down_ref[...].astype(F32)).astype(BF16)
        else:
            to_up[...] = (ahead_ref[...] + up_ref[...].astype(F32)).astype(BF16)
            to_down[...] = (behind_ref[...] + down_ref[...].astype(F32)).astype(BF16)

    operands = (ahead, behind) + (() if up is None else (up, down))
    return run(kernel, operands, [(ahead.shape, BF16)] * 2, after)


def normed_parts(x_ref, gain_ref, inverse, head):
    parts = []
    for start in (head * 2 * HD, head * 2 * HD + HD):
        x = x_ref[:, start : start + HD].astype(F32)
        parts.append((x * inverse * gain_ref[:, start : start + HD]).astype(BF16))
    return parts


def softmax_of(queries, keyvals):
    scores = dot(queries, keyvals, ((1,), (1,))) * SHRINK
    scores = jnp.where(causal(scores.shape[0]), scores, -1e30)
    powers = jnp.exp(scores - jnp.max(scores, axis=-1, keepdims=True))
    return powers / jnp.sum(powers, axis=-1, keepdims=True)


def forward(x, totals, gain, width, after):
    tokens, depth = x.shape

    def kernel(x_ref, gain_ref, *refs):
        total = refs[0][0:1, :]
        for ref in refs[1:-1]:
            total = total + ref[0:1, :]
        inverse = as_column(lax.rsqrt(total / width + EPSILON))
        for head in range(depth // (2 * HD)):
            queries, keyvals = normed_parts(x_ref, gain_ref, inverse, head)
            weights = softmax_of(queries, keyvals).astype(BF16)
            out = dot(weights, keyvals, ((1,), (0,))).astype(BF16)
            refs[-1][:, head * HD : (head + 1) * HD] = out

    return run(kernel, (x, gain, *totals), [((tokens, depth // 2), BF16)], after)[0]


def prepare(x, total, gain, width, after):
    tokens, depth = x.shape
    heads = depth // (2 * HD)

    def kernel(x_ref, total_ref, gain_ref, queries_ref, keyvals_ref, probs_ref):
        inverse = as_column(lax.rsqrt(total_ref[...] / width + EPSILON))
        for head in range(heads):
            queries, keyvals = normed_parts(x_ref, gain_ref, inverse, head)
            at = slice(head * HD, (head + 1) * HD)
            queries_ref[:, at] = queries
            keyvals_ref[:, at] = keyvals
            probs_ref[head] = softmax_of(queries, keyvals)

    results = [((tokens, depth // 2), BF16)] * 2 + [((heads, tokens, tokens), F32)]
    return run(kernel, (x, total, gain), results, after)


def backward(x, gain, queries, keyvals, probs, grads, after):
    tokens, depth = x.shape

    def kernel(x_ref, gain_ref, queries_ref, keyvals_ref, probs_ref, *refs):
        grad_refs, (scaled_ref, moment_ref) = refs[:-2], refs[-2:]
        sums = jnp.zeros((tokens, HD), F32)
        half = tokens // 2
        for head in range(depth // (2 * HD)):
            at = slice(head * HD, (head + 1) * HD)
            queries, keyvals, probs = queries_ref[:, at], keyvals_ref[:, at], probs_ref[head]
            grad = grad_refs[0][:, at]
            if len(grad_refs) > 1 and grad_refs[1].shape[0] == half:
                arrived = jnp.concatenate([ref[:, at] for ref in grad_refs[1:]], axis=0)
                grad = grad + arrived.astype(F32)
            else:
                for ref in grad_refs[1:]:
                    grad = grad + ref[:, at].astype(F32)
            grad = grad.astype(BF16)
            dprob = dot(grad, keyvals, ((1,), (1,)))
            dvalue = dot(probs.astype(BF16), grad, ((0,), (0,)))
            inner = jnp.sum(dprob * probs, axis=-1, keepdims=True)
            dscore = (probs * (dprob - inner) * SHRINK).astype(BF16)
            dquery = dot(dscore, keyvals, ((1,), (0,)))
            dkeyval = dvalue + dot(dscore, queries, ((0,), (0,)))
            for start, value in ((0, dquery), (HD, dkeyval)):
                to = slice(head * 2 * HD + start, head * 2 * HD + start + HD)
                scaled = value * gain_ref[:, to]
                scaled_ref[:, to] = scaled
                sums = sums + scaled * x_ref[:, to].astype(F32)
        moment_ref[...] = as_row(sums)

    results = [((tokens, depth), F32), ((1, tokens), F32)]
    return run(kernel, (x, gain, queries, keyvals, probs, *grads), results, after)


def finish(rows, x, scaled, total, moments, width, after):
    tokens, depth = rows.shape

    def kernel(rows_ref, x_ref, scaled_ref, total_ref, *refs):
        moment = refs[0][...]
        for ref in refs[1:-1]:
            moment = moment + ref[...]
        inverse = lax.rsqrt(total_ref[...] / width + EPSILON)
        pull = as_column(inverse**3 * moment / width)
        inverse = as_column(inverse)
        for start in range(0, depth, HD):
            at = slice(start, start + HD)
            grad = rows_ref[:, at].astype(F32) + inverse * scaled_ref[:, at]
            refs[-1][:, at] = (grad - x_ref[:, at].astype(F32) * pull).astype(BF16)

    operands = (rows, x, scaled, total, *moments)
    return run(kernel, operands, [((tokens, depth), BF16)], after)[0]


def piece(size, most):
    fits = [p for p in range(128, min(size, most) + 1, 128) if size % p == 0]
    return fits[-1] if fits else size


def project(plan, weight, contexts, offsets, chunk, base, after):
    tokens, width = contexts[0].shape[0], weight.shape[1]

    def kernel(weight_ref, *refs):
        total = None
        for context, offset in zip(refs, offsets):
            at = first_row(plan, offset, chunk)
            term = dot(context[...], weight_ref[pl.ds(at, chunk), :], ((1,), (0,)))
            total = term if total is None else total + term
        if base is not None:
            total = refs[len(offsets)][...] + total
        refs[-1][...] = total

    operands = (weight, *contexts) + (() if base is None else (base,))
    return run(kernel, operands, [((tokens, width), F32)], after)[0]


def project_last(plan, weight, contexts, offsets, chunk, base, fresh, after):
    tokens, width = fresh.shape
    block = piece(width, 512)
    halves = contexts[0].shape[0] != tokens

    def body(weight_ref, base_ref, fresh_ref, *refs):
        parts, (out_ref, held_ref, sems) = refs[: len(contexts)], refs[-3:]
        copies = []
        for turn, start in enumerate(range(0, width, block)):
            cols = slice(start, start + block)
            if halves:
                at = first_row(plan, offsets[0], chunk)
                weights = weight_ref[pl.ds(at, chunk), cols]
                total = jnp.concatenate([dot(p[...], weights, ((1,), (0,))) for p in parts], axis=0)
            else:
                total = jnp.zeros((tokens, block), F32)
                for context, offset in zip(parts, offsets):
                    at = first_row(plan, offset, chunk)
                    total += dot(context[...], weight_ref[pl.ds(at, chunk), cols], ((1,), (0,)))
            total = fresh_ref[:, cols].astype(F32) + (base_ref[:, cols] + total)
            held_ref[:, cols] = total.astype(BF16)
            copy = pltpu.make_async_copy(held_ref.at[:, cols], out_ref.at[:, cols], sems.at[turn])
            copy.start()
            copies.append(copy)
        for copy in copies:
            copy.wait()

    return pl.pallas_call(
        body,
        in_specs=[VMEM] * (3 + len(contexts) + len(after)),
        out_specs=ANY,
        out_shape=jax.ShapeDtypeStruct((tokens, width), BF16),
        scratch_shapes=[
            pltpu.VMEM((tokens, width), BF16),
            pltpu.SemaphoreType.DMA((width // block,)),
        ],
        compiler_params=pltpu.CompilerParams(vmem_limit_bytes=ROOM),
        name="last",
    )(weight, base, fresh, *contexts, *after)


def mirrored(value):
    sections = lax.axis_size("section")
    return lax.ppermute(value, "section", [(i, sections - 1 - i) for i in range(sections)])


def stages(size):
    stride, found = 1, []
    while stride < size:
        factor = next(f for f in range(2, size + 1) if (size // stride) % f == 0)
        found.append((stride, factor))
        stride *= factor
    return found


def exchanged(value, stage, size):
    stride, factor = stage
    terms = [value]
    for turn in range(1, factor):
        pairs = []
        for i in range(size):
            digit = (i // stride) % factor
            pairs.append((i, i + ((digit + turn) % factor - digit) * stride))
        terms.append(lax.ppermute(value, "fsdp", pairs))
    return terms


def local(order, section_input, stash_held, upstream, norm_gain, out_weight):
    fresh, held, rows = section_input[0], stash_held[0], upstream[0]
    gain, weight = norm_gain, out_weight[0]
    count = len(order)
    tokens = fresh.shape[0]
    width = fresh.shape[1] * count
    chunk = weight.shape[0] // count
    half = tokens // 2
    far = (count - 1) // 2
    opposite = count % 2 == 0
    place = {device: at for at, device in enumerate(order)}
    plan = {
        offset: [order[(place[device] + offset) % count] for device in range(count)]
        for offset in range(-far, count // 2 + 1)
    }
    steps = stages(count)

    def turn(value, step):
        pairs = [(order[i], order[(i + step) % count]) for i in range(count)]
        return lax.ppermute(value, "fsdp", pairs)

    sums, *first = begin(plan, fresh, held, rows, weight, chunk, opposite)
    fetched = mirrored(held)
    up = down = None
    if opposite:
        up = turn(first[0], 1)
        down = turn(first[1], -1 if count > 2 else 1)

    terms = [sums]
    for stage in steps:
        terms = exchanged(functools.reduce(jnp.add, terms), stage, count)
    total_b = mirrored(functools.reduce(jnp.add, [t[1:2] for t in terms]))

    last, context = sums, None
    for distance in range(far, 0, -1):
        pair = partial_sums(plan, rows, weight, (distance, -distance), chunk, (last,))
        last = pair[0]
        if distance == max(far - 1, 1):
            context = forward(fresh, terms, gain, width, (last,))
            last = context
        if distance == 1:
            own = partial_sums(plan, rows, weight, (0,), chunk, (last,))[0]
            last = own
        to_up, to_down = add_arrived(*pair, up, down, (last,))
        last = to_up
        up = turn(to_up, 1)
        down = turn(to_down, -1)
    if far == 0:
        own = partial_sums(plan, rows, weight, (0,), chunk, (last,))[0]
        context = forward(fresh, terms, gain, width, (own,))
    grads = [own] if up is None else [own, up, down]

    queries, keyvals, probs = prepare(fetched, total_b, gain, width, (last,))
    last = queries
    projected = None
    ahead = behind = context
    arrived, offsets = [context], [0]
    scaled = None
    for distance in range(1, far + 1):
        ahead, behind = turn(ahead, 1), turn(behind, -1)
        arrived += [ahead, behind]
        offsets += [-distance, distance]
        if distance < far or opposite:
            projected = project(plan, weight, arrived, offsets, chunk, projected, (last,))
            last = projected
            arrived, offsets = [], []
        if scaled is None:
            scaled, moment = backward(
                fetched, gain, queries, keyvals, probs, grads, (last,)
            )
            last = scaled
    if scaled is None:
        scaled, moment = backward(fetched, gain, queries, keyvals, probs, grads, (last,))
    moments = [moment]
    for stage in steps:
        moments = exchanged(functools.reduce(jnp.add, moments), stage, count)
    grad_in = finish(rows, fetched, scaled, total_b, moments, width, ())
    if projected is None:
        if arrived:
            projected = project(plan, weight, arrived, offsets, chunk, None, ())
            arrived, offsets = [], []
    if opposite:
        ahead = turn(ahead[:half], 1)
        behind = turn(behind[half:], -1 if count > 2 else 1)
        arrived, offsets = [ahead, behind], [count // 2]
    output = project_last(plan, weight, arrived, offsets, chunk, projected, fresh, (grad_in,))
    parked = mirrored(fresh)
    return (output[None], parked[None], grad_in[None])


def solution(mesh):
    order = ring_order(mesh)
    placed = P("section", None, "fsdp")

    def body(*arrays):
        return local(order, *arrays)

    return jax.shard_map(
        body,
        mesh=mesh,
        in_specs=(placed, placed, placed, P("section", "fsdp"), placed),
        out_specs=(placed, placed, placed),
        check_vma=False,
    )
```

time: 253 us -> 116 us (0.46)
  waiting for transfers between devices: 130 us -> 53.7 us
  blocking collectives: 42.3 us -> 0 us
  matrix products: 34.4 us -> 0 us
  starting transfers between devices: 3.5 us -> 29.2 us
  Pallas kernels: 0 us -> 19.7 us
  between operations: 14.2 us -> 0.88 us
  other arithmetic: 11.4 us -> 0.02 us
  local copies, waits for them, and re-layouts: 16.5 us -> 12.6 us
    all_gather x1 -> x0, waiting for transfers between devices: 48.9 us -> none  [local(): lax.all_gather(context_own, 'fsdp', axis=1, tiled=True)]
    reduce_scatter x1 -> x0, waiting for transfers between devices: 47.5 us -> none  [local(): lax.psum_scatter(lax.dot_general(weight_rows, grad_rows, (((1,), (1,)), (...]
    psum x2 -> x0, blocking collectives: 42.3 us -> none  [local(): lax.psum((jnp.sum(fresh_f * fresh_f, axis=-1), jnp.sum(held_f * held_f, a...]
    dot_general x7 -> x0, matrix products: 32 us -> none  [the longest x1 10.9 us: local(): lax.dot_general(weight_rows, grad_rows, (((1,), (1,)), ((), ())), preferr...]
    ppermute x2 -> x25, starting transfers between devices: 3.42 us -> 29.2 us  [the longest x16 19.3 us: turn(): return lax.ppermute(value, 'fsdp', pairs)]
    ppermute x2 -> x25, waiting for transfers between devices: 33.2 us -> 53.7 us  [the longest x16 29.4 us: turn(): return lax.ppermute(value, 'fsdp', pairs)]
    pallas_call x0 -> x16, Pallas kernels: none -> 19.7 us  [the longest x14 15.7 us: run(): pl.pallas_call(body, in_specs=[VMEM] * (len(operands) + len(after)), out_...]
    convert_element_type x3 -> x0, local copies, waits for them, and re-layouts: 7.56 us -> none  [the longest x2 4.55 us: local(): fresh_f = fresh.astype(jnp.float32)]
  transfers between devices with their start and end apart: 4 -> 25, of which waited for: 4 -> 13; matrix products, arithmetic and copies ran while one was open for 9% -> 1% of each run, Pallas kernels for 0% -> 12%
where the time goes in v1:
time: 116 us
  waiting for transfers between devices  53.7 us (46%)
  starting transfers between devices  29.2 us (25%)
  Pallas kernels  19.7 us (17%)
  local copies, waits for them, and re-layouts  12.6 us (11%)
    ppermute x16, waiting for transfers between devices, turn(): return lax.ppermute(value, 'fsdp', pairs)  29.4 us
    ppermute x16, starting transfers between devices, turn(): return lax.ppermute(value, 'fsdp', pairs)  19.3 us
    pallas_call x14, Pallas kernels, run(): pl.pallas_call(body, in_specs=[VMEM] * (len(operands) + len(after)), out_...  15.7 us
    ppermute x3, waiting for transfers between devices, mirrored(): lax.ppermute(value, 'section', [(i, sections - 1 - i) for i in range(sect...  13.3 us
    unnamed x20, local copies, waits for them, and re-layouts  12.5 us
    ppermute x6, waiting for transfers between devices, exchanged(): terms.append(lax.ppermute(value, 'fsdp', pairs))  11.1 us
    ppermute x6, starting transfers between devices, exchanged(): terms.append(lax.ppermute(value, 'fsdp', pairs))  9.88 us
    pallas_call x1, Pallas kernels, begin(): pl.pallas_call(body, in_specs=[ANY] * 4, out_specs=[VMEM] * len(results),...  2.47 us
  transfers between devices with their start and end apart: 25, of which 13 were waited for; matrix products, arithmetic and copies ran while one was open for 1% of the time, Pallas kernels for 12%

profile of v1, /device:TPU:0, one launch (start us, length us, event | category | flops | bytes accessed | tf_op | source)
XLA Modules:
  0.0 116.1 jit_solution(5848222927763791446)
XLA Ops:
  0.6 6.4 %copy-done = bf16[1,6144,1536]{2,1,0:T(8,128)(2,1)S(1)} copy-done((bf16[1,6144,1536]{2,1,0:T(8,128)(2,1)S(1)}, bf16[1,6144,1536]{2,1,0:T(8,128)(2,1)}, u32[]{:S(2)}) %copy-start) | copy-done | bytes 18874392
  10.4 2.5 %begin.1 = (f32[2,256]{1,0:T(2,128)S(1)}, bf16[128,768]{1,0:T(8,128)(2,1)S(1)}, bf16[128,768]{1,0:T(8,128)(2,1)S(1)}) custom-call(bf16[256,1536]{1,0:T(8,128)(2,1)S(1)} %bitcast.23, bf16[256,1536]{1,0:T(8,128)(2,1)S(1)} %bitcast.27, bf16[256,1536]{1,0:T(8,128)(2,1)S(1)} %bitcast.17, bf16[6144,1536]{1,0:T(8,128)(2,1)S(1)} %bitcast.8), custom_call_target="tpu_custom_call" | custom-call | tf_op jit(solution)/shard_map/begin/pallas_call | solution.py:121
  12.9 3.1 %collective-permute-start.3 = (bf16[128,768]{1,0:T(8,128)(2,1)S(1)}, bf16[128,768]{1,0:T(8,128)(2,1)S(1)}, u32[]{:S(2)}, u32[]{:S(2)}) collective-permute-start(bf16[128,768]{1,0:T(8,128)(2,1)S(1)} %get-tuple-element.26), channel_id=1, source_target_pairs={{0,2},{2,4},{4,6},{6,7},{7,5},{5,3},{3,1},{1,0},{8,10},{10,12},{12... | collective-permute-start | bytes 589832 | tf_op jit(solution)/shard_map/ppermute | solution.py:380
  16.0 2.0 %collective-permute-start = (f32[2,256]{1,0:T(2,128)S(1)}, f32[2,256]{1,0:T(2,128)S(1)}, u32[]{:S(2)}, u32[]{:S(2)}) collective-permute-start(f32[2,256]{1,0:T(2,128)S(1)} %get-tuple-element.23.refs_2_), channel_id=1, source_target_pairs={{0,1},{1,0},{2,3},{3,2},{4,5},{5,4},{6,7},{7,6},{8,9},{9,8},{10,11... | collective-permute-start | bytes 6152 | tf_op jit(solution)/shard_map/ppermute | solution.py:357
  17.9 2.9 %collective-permute-done = f32[2,256]{1,0:T(2,128)S(1)} collective-permute-done((f32[2,256]{1,0:T(2,128)S(1)}, f32[2,256]{1,0:T(2,128)S(1)}, u32[]{:S(2)}, u32[]{:S(2)}) %collective-permute-start) | collective-permute-done | bytes 2080 | tf_op jit(solution)/shard_map/ppermute | solution.py:357
  21.6 2.9 %collective-permute-done.1 = f32[2,256]{1,0:T(2,128)S(1)} collective-permute-done((f32[2,256]{1,0:T(2,128)S(1)}, f32[2,256]{1,0:T(2,128)S(1)}, u32[]{:S(2)}, u32[]{:S(2)}) %collective-permute-start.1) | collective-permute-done | bytes 2080 | tf_op jit(solution)/shard_map/ppermute | solution.py:357
  24.5 3.6 %collective-permute-start.2 = (f32[2,256]{1,0:T(2,128)S(1)}, f32[2,256]{1,0:T(2,128)S(1)}, u32[]{:S(2)}, u32[]{:S(2)}) collective-permute-start(f32[2,256]{1,0:T(2,128)S(1)} %add.16.refs_2_), channel_id=1, source_target_pairs={{0,4},{1,5},{2,6},{3,7},{4,0},{5,1},{6,2},{7,3},{8,12},{9,13},{10,... | collective-permute-start | bytes 6152 | tf_op jit(solution)/shard_map/ppermute | solution.py:357
  28.1 1.4 %shard_map.76 = (f32[256,768]{1,0:T(8,128)S(1)}, f32[256,768]{1,0:T(8,128)S(1)}) custom-call(bf16[256,1536]{1,0:T(8,128)(2,1)S(1)} %bitcast.18, bf16[6144,1536]{1,0:T(8,128)(2,1)S(1)} %bitcast.9, f32[2,256]{1,0:T(2,128)S(1)} %get-tuple-element.23.refs_2_), custom_call_target="tpu_custom_call" | custom-call | tf_op jit(solution)/shard_map/pallas_call | solution.py:49
  30.6 1.4 %shard_map.78 = (f32[256,768]{1,0:T(8,128)S(1)}, f32[256,768]{1,0:T(8,128)S(1)}) custom-call(bf16[256,1536]{1,0:T(8,128)(2,1)S(1)} %bitcast.19, bf16[6144,1536]{1,0:T(8,128)(2,1)S(1)} %bitcast.10, bf16[256,768]{1,0:T(8,128)(2,1)S(1)} %get-tuple-element.28.refs_2_), custom_call_target="tpu_custom_call" | custom-call | tf_op jit(solution)/shard_map/pallas_call | solution.py:49
  32.1 1.4 %shard_map.79.refs_4_.refs_1_ = bf16[256,768]{1,0:T(8,128)(2,1)S(1)} custom-call(bf16[256,1536]{1,0:T(8,128)(2,1)S(1)} %bitcast.24, f32[1,1536]{1,0:T(1,128)S(1)} %copy-done.8, f32[2,256]{1,0:T(2,128)S(1)} %add.16.refs_2_, f32[2,256]{1,0:T(2,128)S(1)} %collective-permute-done.2.refs_3_, f32[256,768]{1,0:T(8,128)S(1)} %get-tuple-element.29.refs_4_.refs_0_), custom_call_target="tpu_custom_call" | custom-call | tf_op jit(solution)/shard_map/pallas_call | solution.py:49
  33.9 1.8 %collective-permute-start.13 = (bf16[256,768]{1,0:T(8,128)(2,1)S(1)}, bf16[256,768]{1,0:T(8,128)(2,1)S(1)}, u32[]{:S(2)}, u32[]{:S(2)}) collective-permute-start(bf16[256,768]{1,0:T(8,128)(2,1)S(1)} %get-tuple-element.28.refs_2_), channel_id=1, source_target_pairs={{0,2},{2,4},{4,6},{6,7},{7,5},{5,3},{3,1},{1,0},{8,10},{10,12},{12... | collective-permute-start | bytes 1179656 | tf_op jit(solution)/shard_map/ppermute | solution.py:380
  35.9 1.8 %collective-permute-start.5 = (bf16[256,768]{1,0:T(8,128)(2,1)S(1)}, bf16[256,768]{1,0:T(8,128)(2,1)S(1)}, u32[]{:S(2)}, u32[]{:S(2)}) collective-permute-start(bf16[256,768]{1,0:T(8,128)(2,1)S(1)} %shard_map.79.refs_4_.refs_1_), channel_id=1, source_target_pairs={{0,2},{2,4},{4,6},{6,7},{7,5},{5,3},{3,1},{1,0},{8,10},{10,12},{12... | collective-permute-start | bytes 1179656 | tf_op jit(solution)/shard_map/ppermute | solution.py:380
  37.7 7.9 %collective-permute-done.8.refs_3_ = bf16[256,768]{1,0:T(8,128)(2,1)S(1)} collective-permute-done((bf16[256,768]{1,0:T(8,128)(2,1)S(1)}, bf16[256,768]{1,0:T(8,128)(2,1)S(1)}, u32[]{:S(2)}, u32[]{:S(2)}) %collective-permute-start.8) | collective-permute-done | bytes 393248 | tf_op jit(solution)/shard_map/ppermute | solution.py:380
  45.9 8.1 %collective-permute-done.14.refs_3_ = bf16[256,768]{1,0:T(8,128)(2,1)S(1)} collective-permute-done((bf16[256,768]{1,0:T(8,128)(2,1)S(1)}, bf16[256,768]{1,0:T(8,128)(2,1)S(1)}, u32[]{:S(2)}, u32[]{:S(2)}) %collective-permute-start.14) | collective-permute-done | bytes 393248 | tf_op jit(solution)/shard_map/ppermute | solution.py:380
  54.1 2.1 %collective-permute-start.15 = (bf16[256,768]{1,0:T(8,128)(2,1)S(1)}, bf16[256,768]{1,0:T(8,128)(2,1)S(1)}, u32[]{:S(2)}, u32[]{:S(2)}) collective-permute-start(bf16[256,768]{1,0:T(8,128)(2,1)S(1)} %get-tuple-element.32.refs_2_), channel_id=1, source_target_pairs={{0,2},{2,4},{4,6},{6,7},{7,5},{5,3},{3,1},{1,0},{8,10},{10,12},{12... | collective-permute-start | bytes 1179656 | tf_op jit(solution)/shard_map/ppermute | solution.py:380
  56.3 1.9 %collective-permute-start.16 = (bf16[256,768]{1,0:T(8,128)(2,1)S(1)}, bf16[256,768]{1,0:T(8,128)(2,1)S(1)}, u32[]{:S(2)}, u32[]{:S(2)}) collective-permute-start(bf16[256,768]{1,0:T(8,128)(2,1)S(1)} %get-tuple-element.35), channel_id=1, source_target_pairs={{0,1},{2,0},{4,2},{6,4},{7,6},{5,7},{3,5},{1,3},{8,9},{10,8},{12,1... | collective-permute-start | bytes 1179656 | tf_op jit(solution)/shard_map/ppermute | solution.py:380
  59.6 3.9 %collective-permute-done.15.refs_2_ = bf16[256,768]{1,0:T(8,128)(2,1)S(1)} collective-permute-done((bf16[256,768]{1,0:T(8,128)(2,1)S(1)}, bf16[256,768]{1,0:T(8,128)(2,1)S(1)}, u32[]{:S(2)}, u32[]{:S(2)}) %collective-permute-start.15) | collective-permute-done | bytes 393248 | tf_op jit(solution)/shard_map/ppermute | solution.py:380
  63.5 4.2 %collective-permute-done.6.refs_1_ = bf16[256,768]{1,0:T(8,128)(2,1)S(1)} collective-permute-done((bf16[256,768]{1,0:T(8,128)(2,1)S(1)}, bf16[256,768]{1,0:T(8,128)(2,1)S(1)}, u32[]{:S(2)}, u32[]{:S(2)}) %collective-permute-start.6) | collective-permute-done | bytes 393248 | tf_op jit(solution)/shard_map/ppermute | solution.py:380
  67.7 1.5 %collective-permute-start.7 = (bf16[256,768]{1,0:T(8,128)(2,1)S(1)}, bf16[256,768]{1,0:T(8,128)(2,1)S(1)}, u32[]{:S(2)}, u32[]{:S(2)}) collective-permute-start(bf16[256,768]{1,0:T(8,128)(2,1)S(1)} %collective-permute-done.6.refs_1_), channel_id=1, source_target_pairs={{0,2},{2,4},{4,6},{6,7},{7,5},{5,3},{3,1},{1,0},{8,10},{10,12},{12... | collective-permute-start | bytes 1179656 | tf_op jit(solution)/shard_map/ppermute | solution.py:380
  69.2 1.4 %shard_map.81 = (f32[256,768]{1,0:T(8,128)S(1)}, f32[256,768]{1,0:T(8,128)S(1)}) custom-call(bf16[256,1536]{1,0:T(8,128)(2,1)S(1)} %bitcast.20, bf16[6144,1536]{1,0:T(8,128)(2,1)S(1)} %bitcast.11, bf16[256,768]{1,0:T(8,128)(2,1)S(1)} %get-tuple-element.32.refs_2_), custom_call_target="tpu_custom_call" | custom-call | tf_op jit(solution)/shard_map/pallas_call | solution.py:49
  71.7 1.7 %collective-permute-start.17 = (bf16[256,768]{1,0:T(8,128)(2,1)S(1)}, bf16[256,768]{1,0:T(8,128)(2,1)S(1)}, u32[]{:S(2)}, u32[]{:S(2)}) collective-permute-start(bf16[256,768]{1,0:T(8,128)(2,1)S(1)} %get-tuple-element.36.refs_3_), channel_id=1, source_target_pairs={{0,2},{2,4},{4,6},{6,7},{7,5},{5,3},{3,1},{1,0},{8,10},{10,12},{12... | collective-permute-start | bytes 1179656 | tf_op jit(solution)/shard_map/ppermute | solution.py:380
  73.4 2.8 %collective-permute-done.10.refs_2_ = bf16[256,768]{1,0:T(8,128)(2,1)S(1)} collective-permute-done((bf16[256,768]{1,0:T(8,128)(2,1)S(1)}, bf16[256,768]{1,0:T(8,128)(2,1)S(1)}, u32[]{:S(2)}, u32[]{:S(2)}) %collective-permute-start.10) | collective-permute-done | bytes 393248 | tf_op jit(solution)/shard_map/ppermute | solution.py:380
  76.2 1.8 %collective-permute-start.18 = (bf16[256,768]{1,0:T(8,128)(2,1)S(1)}, bf16[256,768]{1,0:T(8,128)(2,1)S(1)}, u32[]{:S(2)}, u32[]{:S(2)}) collective-permute-start(bf16[256,768]{1,0:T(8,128)(2,1)S(1)} %get-tuple-element.40), channel_id=1, source_target_pairs={{0,1},{2,0},{4,2},{6,4},{7,6},{5,7},{3,5},{1,3},{8,9},{10,8},{12,1... | collective-permute-start | bytes 1179656 | tf_op jit(solution)/shard_map/ppermute | solution.py:380
  78.0 1.7 %collective-permute-done.7.refs_1_ = bf16[256,768]{1,0:T(8,128)(2,1)S(1)} collective-permute-done((bf16[256,768]{1,0:T(8,128)(2,1)S(1)}, bf16[256,768]{1,0:T(8,128)(2,1)S(1)}, u32[]{:S(2)}, u32[]{:S(2)}) %collective-permute-start.7) | collective-permute-done | bytes 393248 | tf_op jit(solution)/shard_map/ppermute | solution.py:380
  79.7 13.3 %collective-permute-done.12.refs_1_.refs_3_ = f32[1,256]{1,0:T(1,128)S(1)} collective-permute-done((f32[1,256]{1,0:T(1,128)S(1)}, f32[1,256]{1,0:T(1,128)S(1)}, u32[]{:S(2)}, u32[]{:S(2)}) %collective-permute-start.12) | collective-permute-done | bytes 1056 | tf_op jit(solution)/shard_map/ppermute | solution.py:337
  95.9 2.0 %shard_map.85.refs_8_.refs_3_ = f32[256,1536]{1,0:T(8,128)S(1)} custom-call(bf16[6144,1536]{1,0:T(8,128)(2,1)S(1)} %bitcast.13, bf16[256,768]{1,0:T(8,128)(2,1)S(1)} %shard_map.79.refs_4_.refs_1_, bf16[256,768]{1,0:T(8,128)(2,1)S(1)} %collective-permute-done.5.refs_2_, bf16[256,768]{1,0:T(8,128)(2,1)S(1)} %collective-permute-done.8.refs_3_, ...), custom_call_target="tpu_custom_call" | custom-call | tf_op jit(solution)/shard_map/pallas_call | solution.py:49
  97.9 2.6 %shard_map.86 = (f32[256,1536]{1,0:T(8,128)S(1)}, f32[1,256]{1,0:T(1,128)S(1)}) custom-call(bf16[256,1536]{1,0:T(8,128)(2,1)S(1)} %collective-permute-done.11.refs_0_.refs_1_, f32[1,1536]{1,0:T(1,128)S(1)} %copy-done.8, bf16[256,768]{1,0:T(8,128)(2,1)S(1)} %get-tuple-element.37.refs_4_.refs_2_, bf16[256,768]{1,0:T(8,128)(2,1)S(1)} %get-tuple-element.38.refs_3_, ...), custom_call_target="tpu_custom_call" | custom-call | tf_op jit(solution)/shard_map/pallas_call | solution.py:49
  100.5 2.0 %collective-permute-start.21 = (f32[1,256]{1,0:T(1,128)S(1)}, f32[1,256]{1,0:T(1,128)S(1)}, u32[]{:S(2)}, u32[]{:S(2)}) collective-permute-start(f32[1,256]{1,0:T(1,128)S(1)} %get-tuple-element.42), channel_id=1, source_target_pairs={{0,1},{1,0},{2,3},{3,2},{4,5},{5,4},{6,7},{7,6},{8,9},{9,8},{10,11... | collective-permute-start | bytes 3080 | tf_op jit(solution)/shard_map/ppermute | solution.py:357
  102.5 1.6 %collective-permute-done.21 = f32[1,256]{1,0:T(1,128)S(1)} collective-permute-done((f32[1,256]{1,0:T(1,128)S(1)}, f32[1,256]{1,0:T(1,128)S(1)}, u32[]{:S(2)}, u32[]{:S(2)}) %collective-permute-start.21) | collective-permute-done | bytes 1056 | tf_op jit(solution)/shard_map/ppermute | solution.py:357
  105.1 2.6 %collective-permute-done.22 = f32[1,256]{1,0:T(1,128)S(1)} collective-permute-done((f32[1,256]{1,0:T(1,128)S(1)}, f32[1,256]{1,0:T(1,128)S(1)}, u32[]{:S(2)}, u32[]{:S(2)}) %collective-permute-start.22) | collective-permute-done | bytes 1056 | tf_op jit(solution)/shard_map/ppermute | solution.py:357
  109.8 1.4 %shard_map.88.base_ref = f32[256,1536]{1,0:T(8,128)S(1)} custom-call(bf16[6144,1536]{1,0:T(8,128)(2,1)S(1)} %bitcast.15, bf16[256,768]{1,0:T(8,128)(2,1)S(1)} %collective-permute-done.7.refs_1_, bf16[256,768]{1,0:T(8,128)(2,1)S(1)} %collective-permute-done.10.refs_2_, f32[256,1536]{1,0:T(8,128)S(1)} %shard_map.87.refs_3_.refs_4_, ...), custom_call_target="tpu_custom_call" | custom-call | tf_op jit(solution)/shard_map/pallas_call | solution.py:49
  113.6 1.6 %last.1 = bf16[256,1536]{1,0:T(8,128)(2,1)} custom-call(bf16[6144,1536]{1,0:T(8,128)(2,1)S(1)} %bitcast.16, f32[256,1536]{1,0:T(8,128)S(1)} %shard_map.88.base_ref, bf16[256,1536]{1,0:T(8,128)(2,1)S(1)} %bitcast.26, bf16[128,768]{1,0:T(8,128)(2,1)S(1)} %collective-permute-done.19.refs_0_, bf16[128,768]{1,0:T(8,128)(2,1)S(1)} %collective-permute-done.20.refs_1_, ...), custom_call_target="tpu_custom_call" | custom-call | tf_op jit(solution)/shard_map/last/pallas_call | solution.py:321
  (61 shorter events, 17.8 us)
Async XLA Ops:
  0.6 6.4 %copy-start = (bf16[1,6144,1536]{2,1,0:T(8,128)(2,1)S(1)}, bf16[1,6144,1536]{2,1,0:T(8,128)(2,1)}, u32[]{:S(2)}) copy-start(bf16[1,6144,1536]{2,1,0:T(8,128)(2,1)} %param.9) | copy-start | bytes 56623108
  7.0 1.1 copy-start.2
  10.4 17.7 %copy-start.1 = (bf16[1,6144,1536]{2,1,0:T(8,128)(2,1)S(1)}, bf16[1,6144,1536]{2,1,0:T(8,128)(2,1)}, u32[]{:S(2)}) copy-start(bf16[1,6144,1536]{2,1,0:T(8,128)(2,1)} %param.9) | copy-start | bytes 56623108
  12.9 16.6 %collective-permute-start.3 = (bf16[128,768]{1,0:T(8,128)(2,1)S(1)}, bf16[128,768]{1,0:T(8,128)(2,1)S(1)}, u32[]{:S(2)}, u32[]{:S(2)}) collective-permute-start(bf16[128,768]{1,0:T(8,128)(2,1)S(1)} %get-tuple-element.26), channel_id=1, source_target_pairs={{0,2},{2,4},{4,6},{6,7},{7,5},{5,3},{3,1},{1,0},{8,10},{10,12},{12... | collective-permute-start | bytes 589832 | tf_op jit(solution)/shard_map/ppermute | solution.py:380
  16.0 13.5 %collective-permute-start.4 = (bf16[128,768]{1,0:T(8,128)(2,1)S(1)}, bf16[128,768]{1,0:T(8,128)(2,1)S(1)}, u32[]{:S(2)}, u32[]{:S(2)}) collective-permute-start(bf16[128,768]{1,0:T(8,128)(2,1)S(1)} %get-tuple-element.27), channel_id=1, source_target_pairs={{0,1},{2,0},{4,2},{6,4},{7,6},{5,7},{3,5},{1,3},{8,9},{10,8},{12,1... | collective-permute-start | bytes 589832 | tf_op jit(solution)/shard_map/ppermute | solution.py:380
  16.0 4.9 %collective-permute-start = (f32[2,256]{1,0:T(2,128)S(1)}, f32[2,256]{1,0:T(2,128)S(1)}, u32[]{:S(2)}, u32[]{:S(2)}) collective-permute-start(f32[2,256]{1,0:T(2,128)S(1)} %get-tuple-element.23.refs_2_), channel_id=1, source_target_pairs={{0,1},{1,0},{2,3},{3,2},{4,5},{5,4},{6,7},{7,6},{8,9},{9,8},{10,11... | collective-permute-start | bytes 6152 | tf_op jit(solution)/shard_map/ppermute | solution.py:357
  20.9 3.6 %collective-permute-start.1 = (f32[2,256]{1,0:T(2,128)S(1)}, f32[2,256]{1,0:T(2,128)S(1)}, u32[]{:S(2)}, u32[]{:S(2)}) collective-permute-start(f32[2,256]{1,0:T(2,128)S(1)} %add.15), channel_id=1, source_target_pairs={{0,2},{1,3},{2,0},{3,1},{4,6},{5,7},{6,4},{7,5},{8,10},{9,11},{10,... | collective-permute-start | bytes 6152 | tf_op jit(solution)/shard_map/ppermute | solution.py:357
  24.5 7.6 %collective-permute-start.2 = (f32[2,256]{1,0:T(2,128)S(1)}, f32[2,256]{1,0:T(2,128)S(1)}, u32[]{:S(2)}, u32[]{:S(2)}) collective-permute-start(f32[2,256]{1,0:T(2,128)S(1)} %add.16.refs_2_), channel_id=1, source_target_pairs={{0,4},{1,5},{2,6},{3,7},{4,0},{5,1},{6,2},{7,3},{8,12},{9,13},{10,... | collective-permute-start | bytes 6152 | tf_op jit(solution)/shard_map/ppermute | solution.py:357
  29.5 1.1 copy-start.3
  30.6 1.5 %copy-start.5 = (bf16[1,256,1536]{2,1,0:T(8,128)(2,1)S(1)}, bf16[1,256,1536]{2,1,0:T(8,128)(2,1)}, u32[]{:S(2)}) copy-start(bf16[1,256,1536]{2,1,0:T(8,128)(2,1)} %param.5) | copy-start | bytes 2359300
  30.6 1.5 %copy-start.8 = (f32[1,1536]{1,0:T(1,128)S(1)}, f32[1,1536]{1,0:T(1,128)}, u32[]{:S(2)}) copy-start(f32[1,1536]{1,0:T(1,128)} %refs_1_.3) | copy-start | bytes 18436
  33.5 22.8 %copy-start.7 = (bf16[1,256,1536]{2,1,0:T(8,128)(2,1)S(1)}, bf16[1,256,1536]{2,1,0:T(8,128)(2,1)}, u32[]{:S(2)}) copy-start(bf16[1,256,1536]{2,1,0:T(8,128)(2,1)} %param.6) | copy-start | bytes 2359300
  33.5 12.0 %collective-permute-start.8 = (bf16[256,768]{1,0:T(8,128)(2,1)S(1)}, bf16[256,768]{1,0:T(8,128)(2,1)S(1)}, u32[]{:S(2)}, u32[]{:S(2)}) collective-permute-start(bf16[256,768]{1,0:T(8,128)(2,1)S(1)} %shard_map.79.refs_4_.refs_1_), channel_id=1, source_target_pairs={{0,1},{2,0},{4,2},{6,4},{7,6},{5,7},{3,5},{1,3},{8,9},{10,8},{12,1... | collective-permute-start | bytes 1179656 | tf_op jit(solution)/shard_map/ppermute | solution.py:380
  33.9 12.0 %collective-permute-start.13 = (bf16[256,768]{1,0:T(8,128)(2,1)S(1)}, bf16[256,768]{1,0:T(8,128)(2,1)S(1)}, u32[]{:S(2)}, u32[]{:S(2)}) collective-permute-start(bf16[256,768]{1,0:T(8,128)(2,1)S(1)} %get-tuple-element.28.refs_2_), channel_id=1, source_target_pairs={{0,2},{2,4},{4,6},{6,7},{7,5},{5,3},{3,1},{1,0},{8,10},{10,12},{12... | collective-permute-start | bytes 1179656 | tf_op jit(solution)/shard_map/ppermute | solution.py:380
  35.7 18.3 %collective-permute-start.14 = (bf16[256,768]{1,0:T(8,128)(2,1)S(1)}, bf16[256,768]{1,0:T(8,128)(2,1)S(1)}, u32[]{:S(2)}, u32[]{:S(2)}) collective-permute-start(bf16[256,768]{1,0:T(8,128)(2,1)S(1)} %get-tuple-element.31), channel_id=1, source_target_pairs={{0,1},{2,0},{4,2},{6,4},{7,6},{5,7},{3,5},{1,3},{8,9},{10,8},{12,1... | collective-permute-start | bytes 1179656 | tf_op jit(solution)/shard_map/ppermute | solution.py:380
  35.9 20.3 %collective-permute-start.5 = (bf16[256,768]{1,0:T(8,128)(2,1)S(1)}, bf16[256,768]{1,0:T(8,128)(2,1)S(1)}, u32[]{:S(2)}, u32[]{:S(2)}) collective-permute-start(bf16[256,768]{1,0:T(8,128)(2,1)S(1)} %shard_map.79.refs_4_.refs_1_), channel_id=1, source_target_pairs={{0,2},{2,4},{4,6},{6,7},{7,5},{5,3},{3,1},{1,0},{8,10},{10,12},{12... | collective-permute-start | bytes 1179656 | tf_op jit(solution)/shard_map/ppermute | solution.py:380
  45.6 13.4 %collective-permute-start.9 = (bf16[256,768]{1,0:T(8,128)(2,1)S(1)}, bf16[256,768]{1,0:T(8,128)(2,1)S(1)}, u32[]{:S(2)}, u32[]{:S(2)}) collective-permute-start(bf16[256,768]{1,0:T(8,128)(2,1)S(1)} %collective-permute-done.8.refs_3_), channel_id=1, source_target_pairs={{0,1},{2,0},{4,2},{6,4},{7,6},{5,7},{3,5},{1,3},{8,9},{10,8},{12,1... | collective-permute-start | bytes 1179656 | tf_op jit(solution)/shard_map/ppermute | solution.py:380
  54.1 9.4 %collective-permute-start.15 = (bf16[256,768]{1,0:T(8,128)(2,1)S(1)}, bf16[256,768]{1,0:T(8,128)(2,1)S(1)}, u32[]{:S(2)}, u32[]{:S(2)}) collective-permute-start(bf16[256,768]{1,0:T(8,128)(2,1)S(1)} %get-tuple-element.32.refs_2_), channel_id=1, source_target_pairs={{0,2},{2,4},{4,6},{6,7},{7,5},{5,3},{3,1},{1,0},{8,10},{10,12},{12... | collective-permute-start | bytes 1179656 | tf_op jit(solution)/shard_map/ppermute | solution.py:380
  56.2 11.5 %collective-permute-start.6 = (bf16[256,768]{1,0:T(8,128)(2,1)S(1)}, bf16[256,768]{1,0:T(8,128)(2,1)S(1)}, u32[]{:S(2)}, u32[]{:S(2)}) collective-permute-start(bf16[256,768]{1,0:T(8,128)(2,1)S(1)} %collective-permute-done.5.refs_2_), channel_id=1, source_target_pairs={{0,2},{2,4},{4,6},{6,7},{7,5},{5,3},{3,1},{1,0},{8,10},{10,12},{12... | collective-permute-start | bytes 1179656 | tf_op jit(solution)/shard_map/ppermute | solution.py:380
  56.3 37.7 %collective-permute-start.11 = (bf16[256,1536]{1,0:T(8,128)(2,1)S(1)}, bf16[256,1536]{1,0:T(8,128)(2,1)S(1)}, u32[]{:S(2)}, u32[]{:S(2)}) collective-permute-start(bf16[256,1536]{1,0:T(8,128)(2,1)S(1)} %bitcast.28), channel_id=1, source_target_pairs={{0,24},{8,16},{16,8},{24,0},{1,25},{9,17},{17,9},{25,1},{2,26},{10... | collective-permute-start | bytes 2359304 | tf_op jit(solution)/shard_map/ppermute | solution.py:337
  56.3 15.2 %collective-permute-start.16 = (bf16[256,768]{1,0:T(8,128)(2,1)S(1)}, bf16[256,768]{1,0:T(8,128)(2,1)S(1)}, u32[]{:S(2)}, u32[]{:S(2)}) collective-permute-start(bf16[256,768]{1,0:T(8,128)(2,1)S(1)} %get-tuple-element.35), channel_id=1, source_target_pairs={{0,1},{2,0},{4,2},{6,4},{7,6},{5,7},{3,5},{1,3},{8,9},{10,8},{12,1... | collective-permute-start | bytes 1179656 | tf_op jit(solution)/shard_map/ppermute | solution.py:380
  59.0 17.2 %collective-permute-start.10 = (bf16[256,768]{1,0:T(8,128)(2,1)S(1)}, bf16[256,768]{1,0:T(8,128)(2,1)S(1)}, u32[]{:S(2)}, u32[]{:S(2)}) collective-permute-start(bf16[256,768]{1,0:T(8,128)(2,1)S(1)} %collective-permute-done.9.refs_2_), channel_id=1, source_target_pairs={{0,1},{2,0},{4,2},{6,4},{7,6},{5,7},{3,5},{1,3},{8,9},{10,8},{12,1... | collective-permute-start | bytes 1179656 | tf_op jit(solution)/shard_map/ppermute | solution.py:380
  63.5 44.9 %collective-permute-start.24 = (bf16[256,1536]{1,0:T(8,128)(2,1)S(1)}, bf16[256,1536]{1,0:T(8,128)(2,1)S(1)}, u32[]{:S(2)}, u32[]{:S(2)}) collective-permute-start(bf16[256,1536]{1,0:T(8,128)(2,1)S(1)} %bitcast.25), channel_id=1, source_target_pairs={{0,24},{8,16},{16,8},{24,0},{1,25},{9,17},{17,9},{25,1},{2,26},{10... | collective-permute-start | bytes 2359304 | tf_op jit(solution)/shard_map/ppermute | solution.py:337
  67.7 12.0 %collective-permute-start.7 = (bf16[256,768]{1,0:T(8,128)(2,1)S(1)}, bf16[256,768]{1,0:T(8,128)(2,1)S(1)}, u32[]{:S(2)}, u32[]{:S(2)}) collective-permute-start(bf16[256,768]{1,0:T(8,128)(2,1)S(1)} %collective-permute-done.6.refs_1_), channel_id=1, source_target_pairs={{0,2},{2,4},{4,6},{6,7},{7,5},{5,3},{3,1},{1,0},{8,10},{10,12},{12... | collective-permute-start | bytes 1179656 | tf_op jit(solution)/shard_map/ppermute | solution.py:380
  71.7 26.2 %collective-permute-start.17 = (bf16[256,768]{1,0:T(8,128)(2,1)S(1)}, bf16[256,768]{1,0:T(8,128)(2,1)S(1)}, u32[]{:S(2)}, u32[]{:S(2)}) collective-permute-start(bf16[256,768]{1,0:T(8,128)(2,1)S(1)} %get-tuple-element.36.refs_3_), channel_id=1, source_target_pairs={{0,2},{2,4},{4,6},{6,7},{7,5},{5,3},{3,1},{1,0},{8,10},{10,12},{12... | collective-permute-start | bytes 1179656 | tf_op jit(solution)/shard_map/ppermute | solution.py:380
  76.2 21.7 %collective-permute-start.18 = (bf16[256,768]{1,0:T(8,128)(2,1)S(1)}, bf16[256,768]{1,0:T(8,128)(2,1)S(1)}, u32[]{:S(2)}, u32[]{:S(2)}) collective-permute-start(bf16[256,768]{1,0:T(8,128)(2,1)S(1)} %get-tuple-element.40), channel_id=1, source_target_pairs={{0,1},{2,0},{4,2},{6,4},{7,6},{5,7},{3,5},{1,3},{8,9},{10,8},{12,1... | collective-permute-start | bytes 1179656 | tf_op jit(solution)/shard_map/ppermute | solution.py:380
  79.7 13.3 %collective-permute-start.12 = (f32[1,256]{1,0:T(1,128)S(1)}, f32[1,256]{1,0:T(1,128)S(1)}, u32[]{:S(2)}, u32[]{:S(2)}) collective-permute-start(f32[1,256]{1,0:T(1,128)S(1)} %slice_add_fusion), channel_id=1, source_target_pairs={{0,24},{8,16},{16,8},{24,0},{1,25},{9,17},{17,9},{25,1},{2,26},{10... | collective-permute-start | bytes 3080 | tf_op jit(solution)/shard_map/ppermute | solution.py:337
  93.0 20.6 %collective-permute-start.19 = (bf16[128,768]{1,0:T(8,128)(2,1)S(1)}, bf16[128,768]{1,0:T(8,128)(2,1)S(1)}, u32[]{:S(2)}, u32[]{:S(2)}) collective-permute-start(bf16[128,768]{1,0:T(8,128)(2,1)S(1)} %slice.18), channel_id=1, source_target_pairs={{0,2},{2,4},{4,6},{6,7},{7,5},{5,3},{3,1},{1,0},{8,10},{10,12},{12... | collective-permute-start | bytes 589832 | tf_op jit(solution)/shard_map/ppermute | solution.py:380
  93.9 19.7 %collective-permute-start.20 = (bf16[128,768]{1,0:T(8,128)(2,1)S(1)}, bf16[128,768]{1,0:T(8,128)(2,1)S(1)}, u32[]{:S(2)}, u32[]{:S(2)}) collective-permute-start(bf16[128,768]{1,0:T(8,128)(2,1)S(1)} %slice.19), channel_id=1, source_target_pairs={{0,1},{2,0},{4,2},{6,4},{7,6},{5,7},{3,5},{1,3},{8,9},{10,8},{12,1... | collective-permute-start | bytes 589832 | tf_op jit(solution)/shard_map/ppermute | solution.py:380
  100.5 3.6 %collective-permute-start.21 = (f32[1,256]{1,0:T(1,128)S(1)}, f32[1,256]{1,0:T(1,128)S(1)}, u32[]{:S(2)}, u32[]{:S(2)}) collective-permute-start(f32[1,256]{1,0:T(1,128)S(1)} %get-tuple-element.42), channel_id=1, source_target_pairs={{0,1},{1,0},{2,3},{3,2},{4,5},{5,4},{6,7},{7,6},{8,9},{9,8},{10,11... | collective-permute-start | bytes 3080 | tf_op jit(solution)/shard_map/ppermute | solution.py:357
  104.1 3.6 %collective-permute-start.22 = (f32[1,256]{1,0:T(1,128)S(1)}, f32[1,256]{1,0:T(1,128)S(1)}, u32[]{:S(2)}, u32[]{:S(2)}) collective-permute-start(f32[1,256]{1,0:T(1,128)S(1)} %add.18), channel_id=1, source_target_pairs={{0,2},{1,3},{2,0},{3,1},{4,6},{5,7},{6,4},{7,5},{8,10},{9,11},{10,... | collective-permute-start | bytes 3080 | tf_op jit(solution)/shard_map/ppermute | solution.py:357
  107.7 4.5 %collective-permute-start.23 = (f32[1,256]{1,0:T(1,128)S(1)}, f32[1,256]{1,0:T(1,128)S(1)}, u32[]{:S(2)}, u32[]{:S(2)}) collective-permute-start(f32[1,256]{1,0:T(1,128)S(1)} %add.19.refs_4_), channel_id=1, source_target_pairs={{0,4},{1,5},{2,6},{3,7},{4,0},{5,1},{6,2},{7,3},{8,12},{9,13},{10,... | collective-permute-start | bytes 3080 | tf_op jit(solution)/shard_map/ppermute | solution.py:357
  (2 other events, 2.3 us)

commit v2 on v1

--- a/solution.py
+++ b/solution.py
@@ -10,6 +10,8 @@
 
 HD = 128
 EPSILON = 1e-05
+NARROW = (2, 3, 5)
+WIDE = (4, 2, 3, 5)
 SHRINK = HD ** (-0.5)
 F32 = jnp.float32
 BF16 = jnp.bfloat16
@@ -38,7 +40,7 @@
 
 
 VMEM = pl.BlockSpec(memory_space=pltpu.VMEM)
-ANY = pl.BlockSpec(memory_space=pl.ANY)
+HBM = pl.BlockSpec(memory_space=pltpu.HBM)
 ROOM = 12 * 2**20
 
 
@@ -81,58 +83,74 @@
     return pl.multiple_of(row, chunk)
 
 
-def begin(plan, fresh, held, rows, weight, chunk, opposite):
-    tokens, depth = rows.shape
-    count = len(plan[0])
-
-    def body(fresh_ref, held_ref, rows_ref, weight_ref, *rest):
-        outs, (fresh_v, held_v, rows_v, weight_v, sems) = rest[:-5], rest[-5:]
-        copies = [
-            pltpu.make_async_copy(fresh_ref, fresh_v, sems.at[2]),
-            pltpu.make_async_copy(held_ref, held_v, sems.at[3]),
-        ]
-        if opposite:
-            at = first_row(plan, count // 2, chunk)
-            near = [
-                pltpu.make_async_copy(rows_ref, rows_v, sems.at[0]),
-                pltpu.make_async_copy(weight_ref.at[pl.ds(at, chunk), :], weight_v, sems.at[1]),
-            ]
-            for copy in near:
-                copy.start()
-        for copy in copies:
-            copy.start()
+def squares(fresh, held):
+    tokens, depth = fresh.shape[1:]
+
+    def body(fresh_ref, held_ref, out_ref, fresh_v, held_v, sems):
+        copies = []
+        for slot, (ref, to) in enumerate(((fresh_ref, fresh_v), (held_ref, held_v))):
+            copies.append(pltpu.make_async_copy(ref.at[0], to, sems.at[slot]))
+            copies[-1].start()
         for slot, (copy, ref) in enumerate(zip(copies, (fresh_v, held_v))):
             copy.wait()
             total = jnp.zeros((tokens, HD), F32)
             for start in range(0, depth, HD):
                 part = ref[:, start : start + HD].astype(F32)
                 total = total + part * part
-            outs[0][slot : slot + 1, :] = as_row(total)
-        if opposite:
-            for copy in near:
-                copy.wait()
-            for out, start in zip(outs[1:], (0, tokens // 2)):
-                part = rows_v[start : start + tokens // 2, :]
-                out[...] = dot(part, weight_v[...], ((1,), (1,))).astype(BF16)
-
-    results = [((2, tokens), F32)]
-    if opposite:
-        results += [((tokens // 2, chunk), BF16)] * 2
+            out_ref[slot : slot + 1, :] = as_row(total)
+
     return pl.pallas_call(
         body,
-        in_specs=[ANY] * 4,
-        out_specs=[VMEM] * len(results),
-        out_shape=[pltpu.VMEM(shape, kind) for shape, kind in results],
+        in_specs=[HBM] * 2,
+        out_specs=VMEM,
+        out_shape=pltpu.VMEM((2, tokens), F32),
         scratch_shapes=[
             pltpu.VMEM((tokens, depth), BF16),
             pltpu.VMEM((tokens, depth), BF16),
+            pltpu.SemaphoreType.DMA((2,)),
+        ],
+        compiler_params=pltpu.CompilerParams(vmem_limit_bytes=ROOM),
+        name="squares",
+    )(*(pltpu.with_memory_space_constraint(a, pltpu.HBM) for a in (fresh, held)))
+
+
+def first_halves(plan, rows, weight, offset, chunk, after):
+    tokens, depth = rows.shape[1:]
+    half = tokens // 2
+    block = piece(chunk, 384)
+    pieces = chunk // block
+
+    def body(rows_ref, weight_ref, *refs):
+        up_ref, down_ref, rows_v, weight_v, sems = refs[len(after) :]
+        at = first_row(plan, offset, chunk)
+        copies = [pltpu.make_async_copy(rows_ref.at[0], rows_v, sems.at[0])]
+        for turn in range(pieces):
+            source = weight_ref.at[0, pl.ds(at + turn * block, block), :]
+            to = weight_v.at[pl.ds(turn * block, block), :]
+            copies.append(pltpu.make_async_copy(source, to, sems.at[1 + turn]))
+        for copy in copies:
+            copy.start()
+        copies[0].wait()
+        for turn in range(pieces):
+            copies[1 + turn].wait()
+            cols = slice(turn * block, (turn + 1) * block)
+            part = dot(rows_v[...], weight_v[cols, :], ((1,), (1,))).astype(BF16)
+            up_ref[:, cols] = part[:half]
+            down_ref[:, cols] = part[half:]
+
+    return pl.pallas_call(
+        body,
+        in_specs=[HBM] * 2 + [VMEM] * len(after),
+        out_specs=[VMEM] * 2,
+        out_shape=[pltpu.VMEM((half, chunk), BF16)] * 2,
+        scratch_shapes=[
             pltpu.VMEM((tokens, depth), BF16),
             pltpu.VMEM((chunk, depth), BF16),
-            pltpu.SemaphoreType.DMA((4,)),
+            pltpu.SemaphoreType.DMA((1 + pieces,)),
         ],
         compiler_params=pltpu.CompilerParams(vmem_limit_bytes=ROOM),
-        name="begin",
-    )(fresh, held, rows, weight)
+        name="halves",
+    )(*(pltpu.with_memory_space_constraint(a, pltpu.HBM) for a in (rows, weight)), *after)
 
 
 def partial_sums(plan, rows, weight, offsets, chunk, after):
@@ -250,23 +268,43 @@
     return run(kernel, (x, gain, queries, keyvals, probs, *grads), results, after)
 
 
-def finish(rows, x, scaled, total, moments, width, after):
+def finish(rows, x, scaled, total, moments, width, parked, after):
     tokens, depth = rows.shape
 
-    def kernel(rows_ref, x_ref, scaled_ref, total_ref, *refs):
+    def body(parked_ref, rows_ref, x_ref, scaled_ref, total_ref, *refs):
+        out_ref, moved_ref, held_ref, sems = refs[-4:]
+        copies = [pltpu.make_async_copy(parked_ref, moved_ref, sems.at[0])]
+        copies[0].start()
         moment = refs[0][...]
-        for ref in refs[1:-1]:
+        for ref in refs[1 : len(moments)]:
             moment = moment + ref[...]
         inverse = lax.rsqrt(total_ref[...] / width + EPSILON)
         pull = as_column(inverse**3 * moment / width)
         inverse = as_column(inverse)
-        for start in range(0, depth, HD):
-            at = slice(start, start + HD)
-            grad = rows_ref[:, at].astype(F32) + inverse * scaled_ref[:, at]
-            refs[-1][:, at] = (grad - x_ref[:, at].astype(F32) * pull).astype(BF16)
-
-    operands = (rows, x, scaled, total, *moments)
-    return run(kernel, operands, [((tokens, depth), BF16)], after)[0]
+        for turn, start in enumerate(range(0, depth, 2 * HD)):
+            for part in (start, start + HD):
+                at = slice(part, part + HD)
+                grad = rows_ref[:, at].astype(F32) + inverse * scaled_ref[:, at]
+                held_ref[:, at] = (grad - x_ref[:, at].astype(F32) * pull).astype(BF16)
+            at = slice(start, start + 2 * HD)
+            copy = pltpu.make_async_copy(held_ref.at[:, at], out_ref.at[:, at], sems.at[1 + turn])
+            copy.start()
+            copies.append(copy)
+        for copy in copies:
+            copy.wait()
+
+    return pl.pallas_call(
+        body,
+        in_specs=[VMEM] * (5 + len(moments) + len(after)),
+        out_specs=[HBM, HBM],
+        out_shape=[jax.ShapeDtypeStruct((tokens, depth), BF16)] * 2,
+        scratch_shapes=[
+            pltpu.VMEM((tokens, depth), BF16),
+            pltpu.SemaphoreType.DMA((1 + depth // (2 * HD),)),
+        ],
+        compiler_params=pltpu.CompilerParams(vmem_limit_bytes=ROOM),
+        name="finish",
+    )(parked, rows, x, scaled, total, *moments, *after)
 
 
 def piece(size, most):
@@ -321,7 +359,7 @@
     return pl.pallas_call(
         body,
         in_specs=[VMEM] * (3 + len(contexts) + len(after)),
-        out_specs=ANY,
+        out_specs=HBM,
         out_shape=jax.ShapeDtypeStruct((tokens, width), BF16),
         scratch_shapes=[
             pltpu.VMEM((tokens, width), BF16),
@@ -337,12 +375,12 @@
     return lax.ppermute(value, "section", [(i, sections - 1 - i) for i in range(sections)])
 
 
-def stages(size):
-    stride, found = 1, []
-    while stride < size:
-        factor = next(f for f in range(2, size + 1) if (size // stride) % f == 0)
-        found.append((stride, factor))
-        stride *= factor
+def stages(size, factors):
+    found = []
+    while size > 1:
+        factor = next((f for f in factors if size % f == 0), size)
+        size //= factor
+        found.append((size, factor))
     return found
 
 
@@ -373,31 +411,30 @@
         offset: [order[(place[device] + offset) % count] for device in range(count)]
         for offset in range(-far, count // 2 + 1)
     }
-    steps = stages(count)
 
     def turn(value, step):
         pairs = [(order[i], order[(i + step) % count]) for i in range(count)]
         return lax.ppermute(value, "fsdp", pairs)
 
-    sums, *first = begin(plan, fresh, held, rows, weight, chunk, opposite)
+    sums = squares(section_input, stash_held)
+    last = sums
     fetched = mirrored(held)
     up = down = None
     if opposite:
+        first = first_halves(plan, upstream, out_weight, count // 2, chunk, (last,))
+        last = first[0]
         up = turn(first[0], 1)
         down = turn(first[1], -1 if count > 2 else 1)
 
     terms = [sums]
-    for stage in steps:
+    for stage in stages(count, NARROW):
         terms = exchanged(functools.reduce(jnp.add, terms), stage, count)
     total_b = mirrored(functools.reduce(jnp.add, [t[1:2] for t in terms]))
 
-    last, context = sums, None
+    context = None
     for distance in range(far, 0, -1):
         pair = partial_sums(plan, rows, weight, (distance, -distance), chunk, (last,))
         last = pair[0]
-        if distance == max(far - 1, 1):
-            context = forward(fresh, terms, gain, width, (last,))
-            last = context
         if distance == 1:
             own = partial_sums(plan, rows, weight, (0,), chunk, (last,))[0]
             last = own
@@ -405,6 +442,9 @@
         last = to_up
         up = turn(to_up, 1)
         down = turn(to_down, -1)
+        if distance == far:
+            context = forward(fresh, terms, gain, width, (last,))
+            last = context
     if far == 0:
         own = partial_sums(plan, rows, weight, (0,), chunk, (last,))[0]
         context = forward(fresh, terms, gain, width, (own,))
@@ -432,9 +472,10 @@
     if scaled is None:
         scaled, moment = backward(fetched, gain, queries, keyvals, probs, grads, (last,))
     moments = [moment]
-    for stage in steps:
+    for stage in stages(count, WIDE):
         moments = exchanged(functools.reduce(jnp.add, moments), stage, count)
-    grad_in = finish(rows, fetched, scaled, total_b, moments, width, ())
+    moved = mirrored(fresh)
+    grad_in, parked = finish(rows, fetched, scaled, total_b, moments, width, moved, ())
     if projected is None:
         if arrived:
             projected = project(plan, weight, arrived, offsets, chunk, None, ())
@@ -443,8 +484,7 @@
         ahead = turn(ahead[:half], 1)
         behind = turn(behind[half:], -1 if count > 2 else 1)
         arrived, offsets = [ahead, behind], [count // 2]
-    output = project_last(plan, weight, arrived, offsets, chunk, projected, fresh, (grad_in,))
-    parked = mirrored(fresh)
+    output = project_last(plan, weight, arrived, offsets, chunk, projected, fresh, ())
     return (output[None], parked[None], grad_in[None])
 
 

time: 116 us -> 106 us (0.914)
  local copies, waits for them, and re-layouts: 12.6 us -> 1.47 us
  starting transfers between devices: 29.2 us -> 25.3 us
  Pallas kernels: 19.7 us -> 22.7 us
  waiting for transfers between devices: 53.7 us -> 55.3 us
    unnamed x20 -> x10, local copies, waits for them, and re-layouts: 12.5 us -> 1.45 us
    pallas_call x1 -> x3, Pallas kernels: 2.47 us -> 5.92 us  [the longest x1 2.88 us: first_halves(): pl.pallas_call(body, in_specs=[HBM] * 2 + [VMEM] * len(after), out_specs=...]
    ppermute x16, waiting for transfers between devices: 29.4 us -> 26.4 us  [turn(): return lax.ppermute(value, 'fsdp', pairs)]
    ppermute x6 -> x7, starting transfers between devices: 9.88 us -> 7.37 us  [exchanged(): terms.append(lax.ppermute(value, 'fsdp', pairs))]
    ppermute x3, waiting for transfers between devices: 13.3 us -> 15.6 us  [mirrored(): lax.ppermute(value, 'section', [(i, sections - 1 - i) for i in range(sect...]
    ppermute x6 -> x7, waiting for transfers between devices: 11.1 us -> 13.2 us  [exchanged(): terms.append(lax.ppermute(value, 'fsdp', pairs))]
    ppermute x16, starting transfers between devices: 19.3 us -> 17.5 us  [turn(): return lax.ppermute(value, 'fsdp', pairs)]
    pallas_call x14 -> x13, Pallas kernels: 15.7 us -> 15.2 us  [run(): pl.pallas_call(body, in_specs=[VMEM] * (len(operands) + len(after)), out_...]
  transfers between devices with their start and end apart: 25 -> 26, of which waited for: 13 -> 13; matrix products, arithmetic and copies ran while one was open for 1% -> 0% of each run, Pallas kernels for 12% -> 16%
where the time goes in v2:
time: 106 us
  waiting for transfers between devices  55.3 us (52%)
  starting transfers between devices  25.3 us (24%)
  Pallas kernels  22.7 us (21%)
  local copies, waits for them, and re-layouts  1.47 us (1%)
    ppermute x16, waiting for transfers between devices, turn(): return lax.ppermute(value, 'fsdp', pairs)  26.4 us
    ppermute x16, starting transfers between devices, turn(): return lax.ppermute(value, 'fsdp', pairs)  17.5 us
    ppermute x3, waiting for transfers between devices, mirrored(): lax.ppermute(value, 'section', [(i, sections - 1 - i) for i in range(sect...  15.6 us
    pallas_call x13, Pallas kernels, run(): pl.pallas_call(body, in_specs=[VMEM] * (len(operands) + len(after)), out_...  15.2 us
    ppermute x7, waiting for transfers between devices, exchanged(): terms.append(lax.ppermute(value, 'fsdp', pairs))  13.2 us
    ppermute x7, starting transfers between devices, exchanged(): terms.append(lax.ppermute(value, 'fsdp', pairs))  7.37 us
    pallas_call x1, Pallas kernels, first_halves(): pl.pallas_call(body, in_specs=[HBM] * 2 + [VMEM] * len(after), out_specs=...  2.88 us
  transfers between devices with their start and end apart: 26, of which 13 were waited for; matrix products, arithmetic and copies ran while one was open for 0% of the time, Pallas kernels for 16%

profile of v2, /device:TPU:0, one launch (start us, length us, event | category | flops | bytes accessed | tf_op | source)
XLA Modules:
  0.0 105.7 jit_solution(6407496705325576302)
XLA Ops:
  0.6 1.6 %squares.1.refs_0_ = f32[2,256]{1,0:T(2,128)S(1)} custom-call(bf16[1,256,1536]{2,1,0:T(8,128)(2,1)} %fresh_ref.1, bf16[1,256,1536]{2,1,0:T(8,128)(2,1)} %held_ref.1), custom_call_target="tpu_custom_call" | custom-call | tf_op jit(solution)/shard_map/squares/pallas_call | solution.py:102
  2.3 2.9 %halves.1 = (bf16[128,768]{1,0:T(8,128)(2,1)S(1)}, bf16[128,768]{1,0:T(8,128)(2,1)S(1)}) custom-call(bf16[1,256,1536]{2,1,0:T(8,128)(2,1)} %rows_ref.1, bf16[1,6144,1536]{2,1,0:T(8,128)(2,1)} %weight_ref.1, f32[2,256]{1,0:T(2,128)S(1)} %squares.1.refs_0_), custom_call_target="tpu_custom_call" | custom-call | tf_op jit(solution)/shard_map/halves/pallas_call | solution.py:141
  5.2 3.1 %collective-permute-start.3 = (bf16[128,768]{1,0:T(8,128)(2,1)S(1)}, bf16[128,768]{1,0:T(8,128)(2,1)S(1)}, u32[]{:S(2)}, u32[]{:S(2)}) collective-permute-start(bf16[128,768]{1,0:T(8,128)(2,1)S(1)} %get-tuple-element.24.refs_2_), channel_id=1, source_target_pairs={{0,2},{2,4},{4,6},{6,7},{7,5},{5,3},{3,1},{1,0},{8,10},{10,12},{12... | collective-permute-start | bytes 589832 | tf_op jit(solution)/shard_map/ppermute | solution.py:417
  9.7 1.4 %shard_map.76 = (f32[256,768]{1,0:T(8,128)S(1)}, f32[256,768]{1,0:T(8,128)S(1)}) custom-call(bf16[256,1536]{1,0:T(8,128)(2,1)S(1)} %bitcast.15, bf16[6144,1536]{1,0:T(8,128)(2,1)S(1)} %bitcast.7, bf16[128,768]{1,0:T(8,128)(2,1)S(1)} %get-tuple-element.24.refs_2_), custom_call_target="tpu_custom_call" | custom-call | tf_op jit(solution)/shard_map/pallas_call | solution.py:51
  11.2 1.9 %collective-permute-done.3.refs_2_ = bf16[128,768]{1,0:T(8,128)(2,1)S(1)} collective-permute-done((bf16[128,768]{1,0:T(8,128)(2,1)S(1)}, bf16[128,768]{1,0:T(8,128)(2,1)S(1)}, u32[]{:S(2)}, u32[]{:S(2)}) %collective-permute-start.3) | collective-permute-done | bytes 196640 | tf_op jit(solution)/shard_map/ppermute | solution.py:417
  13.1 1.5 %collective-permute-done.4.refs_3_ = bf16[128,768]{1,0:T(8,128)(2,1)S(1)} collective-permute-done((bf16[128,768]{1,0:T(8,128)(2,1)S(1)}, bf16[128,768]{1,0:T(8,128)(2,1)S(1)}, u32[]{:S(2)}, u32[]{:S(2)}) %collective-permute-start.4) | collective-permute-done | bytes 196640 | tf_op jit(solution)/shard_map/ppermute | solution.py:417
  14.7 1.6 %collective-permute-start.13 = (bf16[256,768]{1,0:T(8,128)(2,1)S(1)}, bf16[256,768]{1,0:T(8,128)(2,1)S(1)}, u32[]{:S(2)}, u32[]{:S(2)}) collective-permute-start(bf16[256,768]{1,0:T(8,128)(2,1)S(1)} %get-tuple-element.28.refs_4_), channel_id=1, source_target_pairs={{0,2},{2,4},{4,6},{6,7},{7,5},{5,3},{3,1},{1,0},{8,10},{10,12},{12... | collective-permute-start | bytes 1179656 | tf_op jit(solution)/shard_map/ppermute | solution.py:417
  16.8 2.6 %collective-permute-start = (f32[2,256]{1,0:T(2,128)S(1)}, f32[2,256]{1,0:T(2,128)S(1)}, u32[]{:S(2)}, u32[]{:S(2)}) collective-permute-start(f32[2,256]{1,0:T(2,128)S(1)} %squares.1.refs_0_), channel_id=1, source_target_pairs={{0,4},{1,5},{2,6},{3,7},{4,0},{5,1},{6,2},{7,3},{8,12},{9,13},{10,... | collective-permute-start | bytes 6152 | tf_op jit(solution)/shard_map/ppermute | solution.py:395
  19.4 7.5 %collective-permute-done = f32[2,256]{1,0:T(2,128)S(1)} collective-permute-done((f32[2,256]{1,0:T(2,128)S(1)}, f32[2,256]{1,0:T(2,128)S(1)}, u32[]{:S(2)}, u32[]{:S(2)}) %collective-permute-start) | collective-permute-done | bytes 2080 | tf_op jit(solution)/shard_map/ppermute | solution.py:395
  26.9 1.5 %collective-permute-start.1 = (f32[2,256]{1,0:T(2,128)S(1)}, f32[2,256]{1,0:T(2,128)S(1)}, u32[]{:S(2)}, u32[]{:S(2)}) collective-permute-start(f32[2,256]{1,0:T(2,128)S(1)} %add.18), channel_id=1, source_target_pairs={{0,2},{1,3},{2,0},{3,1},{4,6},{5,7},{6,4},{7,5},{8,10},{9,11},{10,... | collective-permute-start | bytes 6152 | tf_op jit(solution)/shard_map/ppermute | solution.py:395
  28.4 2.1 %collective-permute-done.1 = f32[2,256]{1,0:T(2,128)S(1)} collective-permute-done((f32[2,256]{1,0:T(2,128)S(1)}, f32[2,256]{1,0:T(2,128)S(1)}, u32[]{:S(2)}, u32[]{:S(2)}) %collective-permute-start.1) | collective-permute-done | bytes 2080 | tf_op jit(solution)/shard_map/ppermute | solution.py:395
  30.6 3.5 %collective-permute-done.2.refs_3_ = f32[2,256]{1,0:T(2,128)S(1)} collective-permute-done((f32[2,256]{1,0:T(2,128)S(1)}, f32[2,256]{1,0:T(2,128)S(1)}, u32[]{:S(2)}, u32[]{:S(2)}) %collective-permute-start.2) | collective-permute-done | bytes 2080 | tf_op jit(solution)/shard_map/ppermute | solution.py:395
  34.1 1.4 %shard_map.78.refs_2_.refs_1_ = bf16[256,768]{1,0:T(8,128)(2,1)S(1)} custom-call(bf16[256,1536]{1,0:T(8,128)(2,1)S(1)} %bitcast.20, f32[1,1536]{1,0:T(1,128)S(1)} %copy-done.3, f32[2,256]{1,0:T(2,128)S(1)} %add.19.refs_2_, f32[2,256]{1,0:T(2,128)S(1)} %collective-permute-done.2.refs_3_, bf16[256,768]{1,0:T(8,128)(2,1)S(1)} %get-tuple-element.28.refs_4_), custom_call_target="tpu_custom_call" | custom-call | tf_op jit(solution)/shard_map/pallas_call | solution.py:51
  35.5 1.6 %collective-permute-start.5 = (bf16[256,768]{1,0:T(8,128)(2,1)S(1)}, bf16[256,768]{1,0:T(8,128)(2,1)S(1)}, u32[]{:S(2)}, u32[]{:S(2)}) collective-permute-start(bf16[256,768]{1,0:T(8,128)(2,1)S(1)} %shard_map.78.refs_2_.refs_1_), channel_id=1, source_target_pairs={{0,2},{2,4},{4,6},{6,7},{7,5},{5,3},{3,1},{1,0},{8,10},{10,12},{12... | collective-permute-start | bytes 1179656 | tf_op jit(solution)/shard_map/ppermute | solution.py:417
  37.6 1.4 %shard_map.79 = (f32[256,768]{1,0:T(8,128)S(1)}, f32[256,768]{1,0:T(8,128)S(1)}) custom-call(bf16[256,1536]{1,0:T(8,128)(2,1)S(1)} %bitcast.16, bf16[6144,1536]{1,0:T(8,128)(2,1)S(1)} %bitcast.8, bf16[256,768]{1,0:T(8,128)(2,1)S(1)} %shard_map.78.refs_2_.refs_1_), custom_call_target="tpu_custom_call" | custom-call | tf_op jit(solution)/shard_map/pallas_call | solution.py:51
  39.2 1.6 %collective-permute-start.15 = (bf16[256,768]{1,0:T(8,128)(2,1)S(1)}, bf16[256,768]{1,0:T(8,128)(2,1)S(1)}, u32[]{:S(2)}, u32[]{:S(2)}) collective-permute-start(bf16[256,768]{1,0:T(8,128)(2,1)S(1)} %get-tuple-element.32.refs_2_), channel_id=1, source_target_pairs={{0,2},{2,4},{4,6},{6,7},{7,5},{5,3},{3,1},{1,0},{8,10},{10,12},{12... | collective-permute-start | bytes 1179656 | tf_op jit(solution)/shard_map/ppermute | solution.py:417
  41.3 6.3 %collective-permute-done.5.refs_2_ = bf16[256,768]{1,0:T(8,128)(2,1)S(1)} collective-permute-done((bf16[256,768]{1,0:T(8,128)(2,1)S(1)}, bf16[256,768]{1,0:T(8,128)(2,1)S(1)}, u32[]{:S(2)}, u32[]{:S(2)}) %collective-permute-start.5) | collective-permute-done | bytes 393248 | tf_op jit(solution)/shard_map/ppermute | solution.py:417
  47.5 1.5 %collective-permute-start.6 = (bf16[256,768]{1,0:T(8,128)(2,1)S(1)}, bf16[256,768]{1,0:T(8,128)(2,1)S(1)}, u32[]{:S(2)}, u32[]{:S(2)}) collective-permute-start(bf16[256,768]{1,0:T(8,128)(2,1)S(1)} %collective-permute-done.5.refs_2_), channel_id=1, source_target_pairs={{0,2},{2,4},{4,6},{6,7},{7,5},{5,3},{3,1},{1,0},{8,10},{10,12},{12... | collective-permute-start | bytes 1179656 | tf_op jit(solution)/shard_map/ppermute | solution.py:417
  49.6 6.4 %collective-permute-done.15.refs_2_ = bf16[256,768]{1,0:T(8,128)(2,1)S(1)} collective-permute-done((bf16[256,768]{1,0:T(8,128)(2,1)S(1)}, bf16[256,768]{1,0:T(8,128)(2,1)S(1)}, u32[]{:S(2)}, u32[]{:S(2)}) %collective-permute-start.15) | collective-permute-done | bytes 393248 | tf_op jit(solution)/shard_map/ppermute | solution.py:417
  56.0 1.5 %collective-permute-done.16.refs_3_ = bf16[256,768]{1,0:T(8,128)(2,1)S(1)} collective-permute-done((bf16[256,768]{1,0:T(8,128)(2,1)S(1)}, bf16[256,768]{1,0:T(8,128)(2,1)S(1)}, u32[]{:S(2)}, u32[]{:S(2)}) %collective-permute-start.16) | collective-permute-done | bytes 393248 | tf_op jit(solution)/shard_map/ppermute | solution.py:417
  57.8 1.4 %shard_map.81 = (f32[256,768]{1,0:T(8,128)S(1)}, f32[256,768]{1,0:T(8,128)S(1)}) custom-call(bf16[256,1536]{1,0:T(8,128)(2,1)S(1)} %bitcast.17, bf16[6144,1536]{1,0:T(8,128)(2,1)S(1)} %bitcast.9, bf16[256,768]{1,0:T(8,128)(2,1)S(1)} %get-tuple-element.32.refs_2_), custom_call_target="tpu_custom_call" | custom-call | tf_op jit(solution)/shard_map/pallas_call | solution.py:51
  60.2 15.6 %collective-permute-done.12.refs_1_.total_ref = f32[1,256]{1,0:T(1,128)S(1)} collective-permute-done((f32[1,256]{1,0:T(1,128)S(1)}, f32[1,256]{1,0:T(1,128)S(1)}, u32[]{:S(2)}, u32[]{:S(2)}) %collective-permute-start.12) | collective-permute-done | bytes 1056 | tf_op jit(solution)/shard_map/ppermute | solution.py:375
  75.8 1.5 %collective-permute-start.17 = (bf16[256,768]{1,0:T(8,128)(2,1)S(1)}, bf16[256,768]{1,0:T(8,128)(2,1)S(1)}, u32[]{:S(2)}, u32[]{:S(2)}) collective-permute-start(bf16[256,768]{1,0:T(8,128)(2,1)S(1)} %get-tuple-element.36.refs_3_), channel_id=1, source_target_pairs={{0,2},{2,4},{4,6},{6,7},{7,5},{5,3},{3,1},{1,0},{8,10},{10,12},{12... | collective-permute-start | bytes 1179656 | tf_op jit(solution)/shard_map/ppermute | solution.py:417
  77.9 1.5 %collective-permute-start.7 = (bf16[256,768]{1,0:T(8,128)(2,1)S(1)}, bf16[256,768]{1,0:T(8,128)(2,1)S(1)}, u32[]{:S(2)}, u32[]{:S(2)}) collective-permute-start(bf16[256,768]{1,0:T(8,128)(2,1)S(1)} %collective-permute-done.6.refs_1_), channel_id=1, source_target_pairs={{0,2},{2,4},{4,6},{6,7},{7,5},{5,3},{3,1},{1,0},{8,10},{10,12},{12... | collective-permute-start | bytes 1179656 | tf_op jit(solution)/shard_map/ppermute | solution.py:417
  80.7 2.0 %shard_map.85.refs_8_.refs_3_ = f32[256,1536]{1,0:T(8,128)S(1)} custom-call(bf16[6144,1536]{1,0:T(8,128)(2,1)S(1)} %bitcast.11, bf16[256,768]{1,0:T(8,128)(2,1)S(1)} %shard_map.78.refs_2_.refs_1_, bf16[256,768]{1,0:T(8,128)(2,1)S(1)} %collective-permute-done.5.refs_2_, bf16[256,768]{1,0:T(8,128)(2,1)S(1)} %collective-permute-done.8.refs_3_, ...), custom_call_target="tpu_custom_call" | custom-call | tf_op jit(solution)/shard_map/pallas_call | solution.py:51
  82.7 5.1 %collective-permute-done.17.refs_6_ = bf16[256,768]{1,0:T(8,128)(2,1)S(1)} collective-permute-done((bf16[256,768]{1,0:T(8,128)(2,1)S(1)}, bf16[256,768]{1,0:T(8,128)(2,1)S(1)}, u32[]{:S(2)}, u32[]{:S(2)}) %collective-permute-start.17) | collective-permute-done | bytes 393248 | tf_op jit(solution)/shard_map/ppermute | solution.py:417
  87.8 1.5 %collective-permute-done.18.refs_7_ = bf16[256,768]{1,0:T(8,128)(2,1)S(1)} collective-permute-done((bf16[256,768]{1,0:T(8,128)(2,1)S(1)}, bf16[256,768]{1,0:T(8,128)(2,1)S(1)}, u32[]{:S(2)}, u32[]{:S(2)}) %collective-permute-start.18) | collective-permute-done | bytes 393248 | tf_op jit(solution)/shard_map/ppermute | solution.py:417
  89.3 2.6 %shard_map.86 = (f32[256,1536]{1,0:T(8,128)S(1)}, f32[1,256]{1,0:T(1,128)S(1)}) custom-call(bf16[256,1536]{1,0:T(8,128)(2,1)S(1)} %collective-permute-done.11.refs_0_.x_ref, f32[1,1536]{1,0:T(1,128)S(1)} %copy-done.3, bf16[256,768]{1,0:T(8,128)(2,1)S(1)} %get-tuple-element.37.refs_4_.refs_2_, bf16[256,768]{1,0:T(8,128)(2,1)S(1)} %get-tuple-element.38.refs_3_, ...), custom_call_target="tpu_custom_call" | custom-call | tf_op jit(solution)/shard_map/pallas_call | solution.py:51
  93.2 2.2 %collective-permute-done.7.refs_1_ = bf16[256,768]{1,0:T(8,128)(2,1)S(1)} collective-permute-done((bf16[256,768]{1,0:T(8,128)(2,1)S(1)}, bf16[256,768]{1,0:T(8,128)(2,1)S(1)}, u32[]{:S(2)}, u32[]{:S(2)}) %collective-permute-start.7) | collective-permute-done | bytes 393248 | tf_op jit(solution)/shard_map/ppermute | solution.py:417
  101.1 1.4 %shard_map.88.base_ref = f32[256,1536]{1,0:T(8,128)S(1)} custom-call(bf16[6144,1536]{1,0:T(8,128)(2,1)S(1)} %bitcast.13, bf16[256,768]{1,0:T(8,128)(2,1)S(1)} %collective-permute-done.7.refs_1_, bf16[256,768]{1,0:T(8,128)(2,1)S(1)} %collective-permute-done.10.refs_2_, f32[256,1536]{1,0:T(8,128)S(1)} %shard_map.87.refs_3_.refs_4_, ...), custom_call_target="tpu_custom_call" | custom-call | tf_op jit(solution)/shard_map/pallas_call | solution.py:51
  102.6 1.4 %finish.1 = (bf16[256,1536]{1,0:T(8,128)(2,1)}, bf16[256,1536]{1,0:T(8,128)(2,1)}) custom-call(bf16[256,1536]{1,0:T(8,128)(2,1)S(1)} %collective-permute-done.21.parked_ref, bf16[256,1536]{1,0:T(8,128)(2,1)S(1)} %bitcast.19, bf16[256,1536]{1,0:T(8,128)(2,1)S(1)} %collective-permute-done.11.refs_0_.x_ref, ...), custom_call_target="tpu_custom_call" | custom-call | tf_op jit(solution)/shard_map/finish/pallas_call | solution.py:296
  104.0 1.6 %last.1 = bf16[256,1536]{1,0:T(8,128)(2,1)} custom-call(bf16[6144,1536]{1,0:T(8,128)(2,1)S(1)} %bitcast.14, f32[256,1536]{1,0:T(8,128)S(1)} %shard_map.88.base_ref, bf16[256,1536]{1,0:T(8,128)(2,1)S(1)} %bitcast.22, bf16[128,768]{1,0:T(8,128)(2,1)S(1)} %collective-permute-done.19.refs_0_, bf16[128,768]{1,0:T(8,128)(2,1)S(1)} %collective-permute-done.20.refs_1_), custom_call_target="tpu_custom_call" | custom-call | tf_op jit(solution)/shard_map/last/pallas_call | solution.py:359
  (53 shorter events, 14.0 us)
Async XLA Ops:
  2.3 7.3 %copy-start = (bf16[1,6144,1536]{2,1,0:T(8,128)(2,1)S(1)}, bf16[1,6144,1536]{2,1,0:T(8,128)(2,1)}, u32[]{:S(2)}) copy-start(bf16[1,6144,1536]{2,1,0:T(8,128)(2,1)} %weight_ref.1) | copy-start | bytes 56623108
  2.3 7.4 %copy-start.1 = (bf16[1,256,1536]{2,1,0:T(8,128)(2,1)S(1)}, bf16[1,256,1536]{2,1,0:T(8,128)(2,1)}, u32[]{:S(2)}) copy-start(bf16[1,256,1536]{2,1,0:T(8,128)(2,1)} %rows_ref.1) | copy-start | bytes 2359300
  5.2 8.0 %collective-permute-start.3 = (bf16[128,768]{1,0:T(8,128)(2,1)S(1)}, bf16[128,768]{1,0:T(8,128)(2,1)S(1)}, u32[]{:S(2)}, u32[]{:S(2)}) collective-permute-start(bf16[128,768]{1,0:T(8,128)(2,1)S(1)} %get-tuple-element.24.refs_2_), channel_id=1, source_target_pairs={{0,2},{2,4},{4,6},{6,7},{7,5},{5,3},{3,1},{1,0},{8,10},{10,12},{12... | collective-permute-start | bytes 589832 | tf_op jit(solution)/shard_map/ppermute | solution.py:417
  8.3 6.4 %collective-permute-start.4 = (bf16[128,768]{1,0:T(8,128)(2,1)S(1)}, bf16[128,768]{1,0:T(8,128)(2,1)S(1)}, u32[]{:S(2)}, u32[]{:S(2)}) collective-permute-start(bf16[128,768]{1,0:T(8,128)(2,1)S(1)} %get-tuple-element.27), channel_id=1, source_target_pairs={{0,1},{2,0},{4,2},{6,4},{7,6},{5,7},{3,5},{1,3},{8,9},{10,8},{12,1... | collective-permute-start | bytes 589832 | tf_op jit(solution)/shard_map/ppermute | solution.py:417
  11.2 19.3 %copy-start.4 = (bf16[1,256,1536]{2,1,0:T(8,128)(2,1)S(1)}, bf16[1,256,1536]{2,1,0:T(8,128)(2,1)}, u32[]{:S(2)}) copy-start(bf16[1,256,1536]{2,1,0:T(8,128)(2,1)} %held_ref.1) | copy-start | bytes 2359300
  11.2 22.9 %copy-start.2 = (bf16[1,256,1536]{2,1,0:T(8,128)(2,1)S(1)}, bf16[1,256,1536]{2,1,0:T(8,128)(2,1)}, u32[]{:S(2)}) copy-start(bf16[1,256,1536]{2,1,0:T(8,128)(2,1)} %fresh_ref.1) | copy-start | bytes 2359300
  11.2 22.9 %copy-start.3 = (f32[1,1536]{1,0:T(1,128)S(1)}, f32[1,1536]{1,0:T(1,128)}, u32[]{:S(2)}) copy-start(f32[1,1536]{1,0:T(1,128)} %refs_1_.3) | copy-start | bytes 18436
  14.7 24.3 %collective-permute-start.13 = (bf16[256,768]{1,0:T(8,128)(2,1)S(1)}, bf16[256,768]{1,0:T(8,128)(2,1)S(1)}, u32[]{:S(2)}, u32[]{:S(2)}) collective-permute-start(bf16[256,768]{1,0:T(8,128)(2,1)S(1)} %get-tuple-element.28.refs_4_), channel_id=1, source_target_pairs={{0,2},{2,4},{4,6},{6,7},{7,5},{5,3},{3,1},{1,0},{8,10},{10,12},{12... | collective-permute-start | bytes 1179656 | tf_op jit(solution)/shard_map/ppermute | solution.py:417
  16.4 22.7 %collective-permute-start.14 = (bf16[256,768]{1,0:T(8,128)(2,1)S(1)}, bf16[256,768]{1,0:T(8,128)(2,1)S(1)}, u32[]{:S(2)}, u32[]{:S(2)}) collective-permute-start(bf16[256,768]{1,0:T(8,128)(2,1)S(1)} %get-tuple-element.31), channel_id=1, source_target_pairs={{0,1},{2,0},{4,2},{6,4},{7,6},{5,7},{3,5},{1,3},{8,9},{10,8},{12,1... | collective-permute-start | bytes 1179656 | tf_op jit(solution)/shard_map/ppermute | solution.py:417
  16.8 10.1 %collective-permute-start = (f32[2,256]{1,0:T(2,128)S(1)}, f32[2,256]{1,0:T(2,128)S(1)}, u32[]{:S(2)}, u32[]{:S(2)}) collective-permute-start(f32[2,256]{1,0:T(2,128)S(1)} %squares.1.refs_0_), channel_id=1, source_target_pairs={{0,4},{1,5},{2,6},{3,7},{4,0},{5,1},{6,2},{7,3},{8,12},{9,13},{10,... | collective-permute-start | bytes 6152 | tf_op jit(solution)/shard_map/ppermute | solution.py:395
  26.9 3.6 %collective-permute-start.1 = (f32[2,256]{1,0:T(2,128)S(1)}, f32[2,256]{1,0:T(2,128)S(1)}, u32[]{:S(2)}, u32[]{:S(2)}) collective-permute-start(f32[2,256]{1,0:T(2,128)S(1)} %add.18), channel_id=1, source_target_pairs={{0,2},{1,3},{2,0},{3,1},{4,6},{5,7},{6,4},{7,5},{8,10},{9,11},{10,... | collective-permute-start | bytes 6152 | tf_op jit(solution)/shard_map/ppermute | solution.py:395
  30.5 3.6 %collective-permute-start.2 = (f32[2,256]{1,0:T(2,128)S(1)}, f32[2,256]{1,0:T(2,128)S(1)}, u32[]{:S(2)}, u32[]{:S(2)}) collective-permute-start(f32[2,256]{1,0:T(2,128)S(1)} %add.19.refs_2_), channel_id=1, source_target_pairs={{0,1},{1,0},{2,3},{3,2},{4,5},{5,4},{6,7},{7,6},{8,9},{9,8},{10,11... | collective-permute-start | bytes 6152 | tf_op jit(solution)/shard_map/ppermute | solution.py:395
  30.5 46.8 %collective-permute-start.11 = (bf16[256,1536]{1,0:T(8,128)(2,1)S(1)}, bf16[256,1536]{1,0:T(8,128)(2,1)S(1)}, u32[]{:S(2)}, u32[]{:S(2)}) collective-permute-start(bf16[256,1536]{1,0:T(8,128)(2,1)S(1)} %bitcast.24), channel_id=1, source_target_pairs={{0,24},{8,16},{16,8},{24,0},{1,25},{9,17},{17,9},{25,1},{2,26},{10... | collective-permute-start | bytes 2359304 | tf_op jit(solution)/shard_map/ppermute | solution.py:375
  35.5 12.0 %collective-permute-start.5 = (bf16[256,768]{1,0:T(8,128)(2,1)S(1)}, bf16[256,768]{1,0:T(8,128)(2,1)S(1)}, u32[]{:S(2)}, u32[]{:S(2)}) collective-permute-start(bf16[256,768]{1,0:T(8,128)(2,1)S(1)} %shard_map.78.refs_2_.refs_1_), channel_id=1, source_target_pairs={{0,2},{2,4},{4,6},{6,7},{7,5},{5,3},{3,1},{1,0},{8,10},{10,12},{12... | collective-permute-start | bytes 1179656 | tf_op jit(solution)/shard_map/ppermute | solution.py:417
  37.1 12.0 %collective-permute-start.8 = (bf16[256,768]{1,0:T(8,128)(2,1)S(1)}, bf16[256,768]{1,0:T(8,128)(2,1)S(1)}, u32[]{:S(2)}, u32[]{:S(2)}) collective-permute-start(bf16[256,768]{1,0:T(8,128)(2,1)S(1)} %shard_map.78.refs_2_.refs_1_), channel_id=1, source_target_pairs={{0,1},{2,0},{4,2},{6,4},{7,6},{5,7},{3,5},{1,3},{8,9},{10,8},{12,1... | collective-permute-start | bytes 1179656 | tf_op jit(solution)/shard_map/ppermute | solution.py:417
  39.2 16.8 %collective-permute-start.15 = (bf16[256,768]{1,0:T(8,128)(2,1)S(1)}, bf16[256,768]{1,0:T(8,128)(2,1)S(1)}, u32[]{:S(2)}, u32[]{:S(2)}) collective-permute-start(bf16[256,768]{1,0:T(8,128)(2,1)S(1)} %get-tuple-element.32.refs_2_), channel_id=1, source_target_pairs={{0,2},{2,4},{4,6},{6,7},{7,5},{5,3},{3,1},{1,0},{8,10},{10,12},{12... | collective-permute-start | bytes 1179656 | tf_op jit(solution)/shard_map/ppermute | solution.py:417
  40.8 16.7 %collective-permute-start.16 = (bf16[256,768]{1,0:T(8,128)(2,1)S(1)}, bf16[256,768]{1,0:T(8,128)(2,1)S(1)}, u32[]{:S(2)}, u32[]{:S(2)}) collective-permute-start(bf16[256,768]{1,0:T(8,128)(2,1)S(1)} %get-tuple-element.35), channel_id=1, source_target_pairs={{0,1},{2,0},{4,2},{6,4},{7,6},{5,7},{3,5},{1,3},{8,9},{10,8},{12,1... | collective-permute-start | bytes 1179656 | tf_op jit(solution)/shard_map/ppermute | solution.py:417
  47.5 30.3 %collective-permute-start.6 = (bf16[256,768]{1,0:T(8,128)(2,1)S(1)}, bf16[256,768]{1,0:T(8,128)(2,1)S(1)}, u32[]{:S(2)}, u32[]{:S(2)}) collective-permute-start(bf16[256,768]{1,0:T(8,128)(2,1)S(1)} %collective-permute-done.5.refs_2_), channel_id=1, source_target_pairs={{0,2},{2,4},{4,6},{6,7},{7,5},{5,3},{3,1},{1,0},{8,10},{10,12},{12... | collective-permute-start | bytes 1179656 | tf_op jit(solution)/shard_map/ppermute | solution.py:417
  49.1 30.3 %collective-permute-start.9 = (bf16[256,768]{1,0:T(8,128)(2,1)S(1)}, bf16[256,768]{1,0:T(8,128)(2,1)S(1)}, u32[]{:S(2)}, u32[]{:S(2)}) collective-permute-start(bf16[256,768]{1,0:T(8,128)(2,1)S(1)} %collective-permute-done.8.refs_3_), channel_id=1, source_target_pairs={{0,1},{2,0},{4,2},{6,4},{7,6},{5,7},{3,5},{1,3},{8,9},{10,8},{12,1... | collective-permute-start | bytes 1179656 | tf_op jit(solution)/shard_map/ppermute | solution.py:417
  56.0 46.6 %collective-permute-start.21 = (bf16[256,1536]{1,0:T(8,128)(2,1)S(1)}, bf16[256,1536]{1,0:T(8,128)(2,1)S(1)}, u32[]{:S(2)}, u32[]{:S(2)}) collective-permute-start(bf16[256,1536]{1,0:T(8,128)(2,1)S(1)} %bitcast.21), channel_id=1, source_target_pairs={{0,24},{8,16},{16,8},{24,0},{1,25},{9,17},{17,9},{25,1},{2,26},{10... | collective-permute-start | bytes 2359304 | tf_op jit(solution)/shard_map/ppermute | solution.py:375
  57.5 18.4 %collective-permute-start.12 = (f32[1,256]{1,0:T(1,128)S(1)}, f32[1,256]{1,0:T(1,128)S(1)}, u32[]{:S(2)}, u32[]{:S(2)}) collective-permute-start(f32[1,256]{1,0:T(1,128)S(1)} %slice_add_fusion), channel_id=1, source_target_pairs={{0,24},{8,16},{16,8},{24,0},{1,25},{9,17},{17,9},{25,1},{2,26},{10... | collective-permute-start | bytes 3080 | tf_op jit(solution)/shard_map/ppermute | solution.py:375
  75.8 12.0 %collective-permute-start.17 = (bf16[256,768]{1,0:T(8,128)(2,1)S(1)}, bf16[256,768]{1,0:T(8,128)(2,1)S(1)}, u32[]{:S(2)}, u32[]{:S(2)}) collective-permute-start(bf16[256,768]{1,0:T(8,128)(2,1)S(1)} %get-tuple-element.36.refs_3_), channel_id=1, source_target_pairs={{0,2},{2,4},{4,6},{6,7},{7,5},{5,3},{3,1},{1,0},{8,10},{10,12},{12... | collective-permute-start | bytes 1179656 | tf_op jit(solution)/shard_map/ppermute | solution.py:417
  77.3 12.0 %collective-permute-start.18 = (bf16[256,768]{1,0:T(8,128)(2,1)S(1)}, bf16[256,768]{1,0:T(8,128)(2,1)S(1)}, u32[]{:S(2)}, u32[]{:S(2)}) collective-permute-start(bf16[256,768]{1,0:T(8,128)(2,1)S(1)} %get-tuple-element.40), channel_id=1, source_target_pairs={{0,1},{2,0},{4,2},{6,4},{7,6},{5,7},{3,5},{1,3},{8,9},{10,8},{12,1... | collective-permute-start | bytes 1179656 | tf_op jit(solution)/shard_map/ppermute | solution.py:417
  77.9 17.5 %collective-permute-start.7 = (bf16[256,768]{1,0:T(8,128)(2,1)S(1)}, bf16[256,768]{1,0:T(8,128)(2,1)S(1)}, u32[]{:S(2)}, u32[]{:S(2)}) collective-permute-start(bf16[256,768]{1,0:T(8,128)(2,1)S(1)} %collective-permute-done.6.refs_1_), channel_id=1, source_target_pairs={{0,2},{2,4},{4,6},{6,7},{7,5},{5,3},{3,1},{1,0},{8,10},{10,12},{12... | collective-permute-start | bytes 1179656 | tf_op jit(solution)/shard_map/ppermute | solution.py:417
  79.4 17.2 %collective-permute-start.10 = (bf16[256,768]{1,0:T(8,128)(2,1)S(1)}, bf16[256,768]{1,0:T(8,128)(2,1)S(1)}, u32[]{:S(2)}, u32[]{:S(2)}) collective-permute-start(bf16[256,768]{1,0:T(8,128)(2,1)S(1)} %collective-permute-done.9.refs_2_), channel_id=1, source_target_pairs={{0,1},{2,0},{4,2},{6,4},{7,6},{5,7},{3,5},{1,3},{8,9},{10,8},{12,1... | collective-permute-start | bytes 1179656 | tf_op jit(solution)/shard_map/ppermute | solution.py:417
  91.9 5.6 %collective-permute-start.22 = (f32[1,256]{1,0:T(1,128)S(1)}, f32[1,256]{1,0:T(1,128)S(1)}, u32[]{:S(2)}, u32[]{:S(2)}) collective-permute-start(f32[1,256]{1,0:T(1,128)S(1)} %get-tuple-element.42), channel_id=1, source_target_pairs={{0,2},{1,3},{2,4},{3,5},{4,6},{5,7},{6,0},{7,1},{8,10},{9,11},{10,... | collective-permute-start | bytes 3080 | tf_op jit(solution)/shard_map/ppermute | solution.py:395
  92.0 6.8 %collective-permute-start.23 = (f32[1,256]{1,0:T(1,128)S(1)}, f32[1,256]{1,0:T(1,128)S(1)}, u32[]{:S(2)}, u32[]{:S(2)}) collective-permute-start(f32[1,256]{1,0:T(1,128)S(1)} %get-tuple-element.42), channel_id=1, source_target_pairs={{0,4},{1,5},{2,6},{3,7},{4,0},{5,1},{6,2},{7,3},{8,12},{9,13},{10,... | collective-permute-start | bytes 3080 | tf_op jit(solution)/shard_map/ppermute | solution.py:395
  95.4 3.6 %collective-permute-start.24 = (f32[1,256]{1,0:T(1,128)S(1)}, f32[1,256]{1,0:T(1,128)S(1)}, u32[]{:S(2)}, u32[]{:S(2)}) collective-permute-start(f32[1,256]{1,0:T(1,128)S(1)} %get-tuple-element.42), channel_id=1, source_target_pairs={{0,6},{1,7},{2,0},{3,1},{4,2},{5,3},{6,4},{7,5},{8,14},{9,15},{10,... | collective-permute-start | bytes 3080 | tf_op jit(solution)/shard_map/ppermute | solution.py:395
  96.6 7.4 %collective-permute-start.19 = (bf16[128,768]{1,0:T(8,128)(2,1)S(1)}, bf16[128,768]{1,0:T(8,128)(2,1)S(1)}, u32[]{:S(2)}, u32[]{:S(2)}) collective-permute-start(bf16[128,768]{1,0:T(8,128)(2,1)S(1)} %slice.18), channel_id=1, source_target_pairs={{0,2},{2,4},{4,6},{6,7},{7,5},{5,3},{3,1},{1,0},{8,10},{10,12},{12... | collective-permute-start | bytes 589832 | tf_op jit(solution)/shard_map/ppermute | solution.py:417
  97.5 6.5 %collective-permute-start.20 = (bf16[128,768]{1,0:T(8,128)(2,1)S(1)}, bf16[128,768]{1,0:T(8,128)(2,1)S(1)}, u32[]{:S(2)}, u32[]{:S(2)}) collective-permute-start(bf16[128,768]{1,0:T(8,128)(2,1)S(1)} %slice.19), channel_id=1, source_target_pairs={{0,1},{2,0},{4,2},{6,4},{7,6},{5,7},{3,5},{1,3},{8,9},{10,8},{12,1... | collective-permute-start | bytes 589832 | tf_op jit(solution)/shard_map/ppermute | solution.py:417
  98.9 3.6 %collective-permute-start.25 = (f32[1,256]{1,0:T(1,128)S(1)}, f32[1,256]{1,0:T(1,128)S(1)}, u32[]{:S(2)}, u32[]{:S(2)}) collective-permute-start(f32[1,256]{1,0:T(1,128)S(1)} %add_add_fusion.refs_0_), channel_id=1, source_target_pairs={{0,1},{1,0},{2,3},{3,2},{4,5},{5,4},{6,7},{7,6},{8,9},{9,8},{10,11... | collective-permute-start | bytes 3080 | tf_op jit(solution)/shard_map/ppermute | solution.py:395
